TPU v7x, 256 devices: a whole 4x4x8 slice. The times are simulated.
256 devices in a mesh: head: 8 (over x, core), blk: 32 (over y, z).
Axes of the slice: x: 4, y: 4, z: 8, core: 2. Of those that a mesh axis runs over, the one named last changes fastest.
Arguments:
- hidden_in: bfloat16 [512, 2048], P('blk', 'head'), may hold values from -6 to 6
- qkv_weight: bfloat16 [2048, 3, 2048], P(None, None, 'head'), may hold values from -0.125 to 0.125
- out_weight: bfloat16 [2048, 2048], P('head'), may hold values from -0.125 to 0.125
- cache_pool: bfloat16 [2048, 64, 2, 2048], P('blk', None, None, 'head'), may hold values from -6 to 6
- page_table: int32 [512, 4], P('blk'), may hold values from 0 to 63, as said below
- request_order: int32 [512], replicated, may hold values from 0 to 511, as said below
- request_lengths: int32 [512], replicated, may hold values from 128 to 256, as said below
- retained_counts: int32 [512], replicated, may hold values from 32 to 128, as said below
- retained_positions: int32 [512, 128], replicated, may hold values from 0 to 255, as said below
- blended_weight: float32 [512, 256], replicated, may hold values from 0.05 to 1
Outputs:
- hidden_out: bfloat16 [512, 2048], P('blk', 'head')
- packed_cache: bfloat16 [512, 132, 2, 2048], P('blk', None, None, 'head')
Inputs may be any that keep to these rules, and one draw needn't show every extreme that they name: `request_order`: a permutation of all 512 positions; of the 16 old positions of one blk index (b * 16 to b * 16 + 15), at most 1 stand at new positions of any one blk index, and exactly 1 at those of some index; the requests at new blk index c come from 16 old blk indices c - k (counted round, k distinct), among which k = 1 and k = 16 always. `page_table`: row r names pool rows counted from the first pool row of blk index r // 16; the 64 pool rows of an index are each named once. `request_lengths`: some request has 256. `retained_counts`: between request_lengths[r] // 4 and request_lengths[r] // 2; some request keeps 128. `retained_positions`: the first retained_counts[r] entries of row r are distinct positions below request_lengths[r], rising; the others are 0.
All inputs are finite; a program needn't handle non-finite values.
Results may differ from a plain program's by a relative error of at most 0.02.
Values may be sent and summed in bfloat16 or wider, within the bound.
No kernel may reach another device: no remote copies, remote signals or barrier semaphores. Data moves between devices by JAX's collectives and lax.ppermute only.
A program may use at most 128 MiB of HBM per device.

v0:
```python
import jax
import jax.numpy as jnp
from jax import lax
from jax.sharding import PartitionSpec as P

HEAD_DIM = 128
PAGE = 64


epsilon = 1e-05


def layer_norm(hidden):
    average = jnp.mean(hidden, axis=-1, keepdims=True)
    centered = hidden - average
    variance = jnp.mean(centered * centered, axis=-1, keepdims=True)
    return centered * lax.rsqrt(variance + epsilon)


def rotate(vectors, positions):
    half_dim = vectors.shape[-1] // 2
    inverse_freq = 10000.0 ** (-jnp.arange(half_dim, dtype=jnp.float32) / half_dim)
    angles = positions.astype(jnp.float32)[:, None, None] * inverse_freq
    cosine = jnp.cos(angles)
    sine_part = jnp.sin(angles)
    first_half = vectors[..., :half_dim]
    second_half = vectors[..., half_dim:]
    return jnp.concatenate(
        [
            first_half * cosine - second_half * sine_part,
            second_half * cosine + first_half * sine_part,
        ],
        axis=-1,
    )


def packing_layout(retain_flags, count_values, length_values, weight_factors):
    kept_total = retain_flags.shape[1]
    capacity_rows = weight_factors.shape[1]
    page_total = capacity_rows // PAGE
    slot_index = jnp.arange(kept_total, dtype=jnp.int32)
    slot_active = slot_index[None, :] < count_values[:, None]
    positions = jnp.arange(capacity_rows, dtype=jnp.int32)
    matches = (retain_flags[:, :, None] == positions[None, None, :]) & slot_active[:, :, None]
    dropped = (positions[None, :] < length_values[:, None]) & jnp.logical_not(
        jnp.any(matches, axis=1)
    )
    dropped_weight = jnp.where(dropped, weight_factors, jnp.zeros((), weight_factors.dtype))
    page_match = (positions // PAGE)[None, :] == jnp.arange(page_total, dtype=jnp.int32)[:, None]
    spread = jnp.where(
        page_match[None], dropped_weight[:, None, :], jnp.zeros((), weight_factors.dtype)
    )
    blending_factors = spread.astype(jnp.bfloat16)
    dropped_mass = jnp.log(1.0 + jnp.sum(spread, axis=2))
    page_live = (jnp.arange(page_total, dtype=jnp.int32) * PAGE)[None, :] < length_values[:, None]
    valid_flags = jnp.concatenate([slot_active, page_live], axis=1)
    logit_bias = jnp.concatenate(
        [jnp.zeros((retain_flags.shape[0], kept_total), weight_factors.dtype), dropped_mass], axis=1
    )
    return (blending_factors, logit_bias, valid_flags, slot_active)


def local(
    hidden_in,
    qkv_weight,
    out_weight,
    cache_pool,
    page_table,
    request_order,
    request_lengths,
    retained_counts,
    retained_positions,
    blended_weight,
):
    rows_here = hidden_in.shape[0]
    model_width = qkv_weight.shape[0]
    head_width = qkv_weight.shape[2]
    heads_here = head_width // HEAD_DIM
    blocks = lax.axis_size("blk")
    capacity = (2 * rows_here + blocks - 1) // blocks
    block_index = lax.axis_index("blk")
    gathered = lax.all_gather(hidden_in, "head", axis=1, tiled=True)
    normed = layer_norm(gathered.astype(jnp.float32)).astype(jnp.bfloat16)
    projections = jnp.dot(
        normed, qkv_weight.reshape(model_width, 3 * head_width), preferred_element_type=jnp.float32
    )
    projections = projections.reshape(rows_here, 3, heads_here, HEAD_DIM)
    local_slots = jnp.arange(rows_here, dtype=jnp.int32)
    own_ids = block_index * rows_here + local_slots
    old_ids = request_order[own_ids]
    positions = request_lengths[old_ids]
    queries = rotate(projections[:, 0], positions).astype(jnp.bfloat16)
    new_keys = rotate(projections[:, 1], positions).astype(jnp.bfloat16)
    new_values = projections[:, 2].astype(jnp.bfloat16)
    total_requests = request_order.shape[0]
    inverse = (
        jnp.zeros((total_requests,), jnp.int32)
        .at[request_order]
        .set(jnp.arange(total_requests, dtype=jnp.int32))
    )
    targets = inverse[own_ids] // rows_here
    earlier = (targets[None, :] == targets[:, None]) & (local_slots[None, :] < local_slots[:, None])
    send_slots = targets * capacity + jnp.sum(earlier.astype(jnp.int32), axis=1)
    sources = old_ids // rows_here
    before = (sources[None, :] == sources[:, None]) & (old_ids[None, :] < old_ids[:, None])
    receive_slots = sources * capacity + jnp.sum(before.astype(jnp.int32), axis=1)
    buffer_rows = blocks * capacity
    slot_source = jnp.zeros((buffer_rows,), jnp.int32).at[send_slots].set(local_slots)
    slot_pages = page_table[slot_source]
    outgoing_pages = cache_pool[slot_pages].reshape(buffer_rows, -1, 2 * head_width)
    landed_layout = packing_layout(
        retained_positions[old_ids],
        retained_counts[old_ids],
        request_lengths[old_ids],
        blended_weight[old_ids],
    )
    arrived = lax.all_to_all(outgoing_pages, "blk", split_axis=0, concat_axis=0, tiled=True)
    landed_keep = retained_positions[old_ids]
    kept_rows = arrived[receive_slots[:, None], landed_keep]
    kept_rows = jnp.where(landed_layout[3][:, :, None], kept_rows, jnp.zeros((), jnp.bfloat16))
    slot_factors = (
        jnp.zeros((buffer_rows,) + landed_layout[0].shape[1:], jnp.bfloat16)
        .at[receive_slots]
        .set(landed_layout[0])
    )
    merged_all = jnp.einsum(
        "rpc,rcx->rpx", slot_factors, arrived, preferred_element_type=jnp.float32
    ).astype(jnp.bfloat16)
    packed = jnp.concatenate([kept_rows, merged_all[receive_slots]], axis=1)
    logit_bias = landed_layout[1]
    valid_flags = landed_layout[2]
    score_scale = HEAD_DIM ** (-0.5)
    key_rows = packed[:, :, :head_width].reshape(rows_here, -1, heads_here, HEAD_DIM)
    value_rows = packed[:, :, head_width:].reshape(rows_here, -1, heads_here, HEAD_DIM)
    scores = (
        jnp.einsum("rhd,rshd->rhs", queries, key_rows, preferred_element_type=jnp.float32)
        * score_scale
        + logit_bias[:, None, :]
    )
    scores = jnp.where(valid_flags[:, None, :], scores, -1e30)
    own_score = (
        jnp.sum(queries.astype(jnp.float32) * new_keys.astype(jnp.float32), axis=-1) * score_scale
    )
    highest = jnp.maximum(jnp.max(scores, axis=-1), own_score)
    exponentials = jnp.exp(scores - highest[:, :, None])
    own_exp = jnp.exp(own_score - highest)
    denominator = jnp.sum(exponentials, axis=-1) + own_exp
    probabilities = (exponentials / denominator[:, :, None]).astype(jnp.bfloat16)
    own_prob = (own_exp / denominator).astype(jnp.bfloat16)
    combined = jnp.einsum(
        "rhs,rshd->rhd", probabilities, value_rows, preferred_element_type=jnp.float32
    )
    combined = combined + own_prob.astype(jnp.float32)[:, :, None] * new_values.astype(jnp.float32)
    attended = combined.astype(jnp.bfloat16).reshape(rows_here, head_width)
    partial_value = jnp.dot(attended, out_weight, preferred_element_type=jnp.float32)
    summed = lax.psum_scatter(
        partial_value.astype(jnp.bfloat16), "head", scatter_dimension=1, tiled=True
    ).astype(jnp.float32)
    hidden_out = (hidden_in.astype(jnp.float32) + summed).astype(jnp.bfloat16)
    packed_cache = packed.reshape(rows_here, -1, 2, head_width)
    return (hidden_out, packed_cache)


def solution(mesh):
    return jax.shard_map(
        local,
        mesh=mesh,
        in_specs=(
            P("blk", "head"),
            P(None, None, "head"),
            P("head", None),
            P("blk", None, None, "head"),
            P("blk", None),
            P(),
            P(),
            P(),
            P(),
            P(),
        ),
        out_specs=(P("blk", "head"), P("blk", None, None, "head")),
        check_vma=False,
    )
```

profile of v0, /device:TPU:1, one launch (start us, length us, event | category | flops | bytes accessed | tf_op | source)
XLA Modules:
  0.0 364.4 jit_solution(1058959069305769532)
XLA Ops:
  8.7 2.4 scatter_custom_fusion
  13.6 21.8 %gather_fusion.5 = bf16[128,64,2,256]{3,2,1,0:T(2,128)(2,1)} fusion(bf16[64,64,2,256]{3,2,1,0:T(2,128)(2,1)} %param.13, s32[1024]{0:T(1024)S(1)} %pad_clamp_fusion.1), kind=kCustom, calls=%fused_computation.5 | custom fusion | bytes 16777728 | tf_op jit(solution)/shard_map/gather | solution.py:110
  35.4 14.0 %reshape.445 = bf16[32,256,512]{2,1,0:T(8,128)(2,1)} reshape(bf16[128,64,2,256]{3,2,1,0:T(2,128)(2,1)} %gather_fusion.5) | data formatting | bytes 16777216 | tf_op jit(solution)/shard_map/reshape | solution.py:110
  49.5 12.3 %all-to-all-start = ((bf16[32,256,512]{2,1,0:T(8,128)(2,1)}), bf16[32,256,512]{2,1,0:T(8,128)(2,1)}, u32[]{:S(2)}, u32[]{:S(2)}) async-start(bf16[32,256,512]{2,1,0:T(8,128)(2,1)} %reshape.445), calls=%async_computation | async-start | bytes 16777216 | tf_op jit(solution)/shard_map/all_to_all | solution.py:117
  62.7 1.5 gather_fusion.6
  65.1 1.6 gather_fusion.8
  67.4 4.7 %copy.27 = bf16[2048,3,256]{0,2,1:T(8,128)(2,1)} copy(bf16[2048,3,256]{2,0,1:T(8,128)(2,1)} %param.11) | data formatting | bytes 6291456 | tf_op args[1]
  73.2 1.0 scatter_fusion
  74.2 14.1 %all_gather.3 = bf16[16,2048]{1,0:T(8,128)(2,1)S(1)} all-gather(bf16[16,256]{1,0:T(8,128)(2,1)S(1)} %copy-done.5), channel_id=1, replica_groups=mesh['head'=8,'blk'=32] {'head'}, dimensions={1}, use_global_device_ids=true | all-gather | bytes 73728 | tf_op jit(solution)/shard_map/all_gather | solution.py:82
  88.7 2.8 fusion.12
  92.1 157.9 %all-to-all-done = bf16[32,256,512]{2,1,0:T(8,128)(2,1)} async-done(((bf16[32,256,512]{2,1,0:T(8,128)(2,1)}), bf16[32,256,512]{2,1,0:T(8,128)(2,1)}, u32[]{:S(2)}, u32[]{:S(2)}) %all-to-all-start) | async-done | bytes 8388640 | tf_op jit(solution)/shard_map/all_to_all | solution.py:117
  250.0 4.6 %convolution_convert_fusion.1 = bf16[32,4,512]{2,1,0:T(4,128)(2,1)S(1)} fusion(bf16[32,4,256]{2,1,0:T(4,128)(2,1)S(1)} %scatter_fusion, bf16[32,256,512]{2,1,0:T(8,128)(2,1)} %all-to-all-done), kind=kOutput, calls=%fused_computation.22 | convolution fusion | flops 33619968 | bytes 8585216 | tf_op jit(solution)/shard_map/rpc,rcx->rpx/dot_general | solution.py:126
  255.2 53.2 %gather_fusion.7 = bf16[2048,512]{1,0:T(8,128)(2,1)S(1)} fusion(bf16[32,256,512]{2,1,0:T(8,128)(2,1)} %all-to-all-done, s32[2048]{0:T(1024)S(1)} %fusion.32), kind=kCustom, calls=%fused_computation.7 | custom fusion | bytes 4210688 | tf_op jit(solution)/shard_map/gather | solution.py:119
  308.5 2.0 gather.56
  310.5 2.6 copy_select_fusion
  313.3 1.1 reshape.447
  314.4 1.2 reshape.446
  315.6 2.1 fusion.4
  318.0 1.8 fusion.2
  319.8 0.9 convolution_convert_fusion
  320.8 5.5 %broadcast_select_fusion = bf16[16,128,2,256]{3,2,1,0:T(2,128)(2,1)S(1)} fusion(bf16[16,128,2,256]{3,2,1,0:T(2,128)(2,1)S(1)} %copy-done.4, pred[16,128]{1,0:T(8,128)(4,1)S(1)} %iota_compare_fusion.3), kind=kLoop, calls=%fused_computation.13 | loop fusion | flops 1048576 | bytes 4196352 | tf_op jit(solution)/shard_map/jit(_where)/select_n | solution.py:120
  326.3 4.1 %pad_maximum_fusion = bf16[16,132,2,256]{3,2,1,0:T(2,128)(2,1)} fusion(bf16[16,4,2,256]{3,2,1,0:T(2,128)(2,1)S(1)} %concatenate.31, bf16[16,128,2,256]{3,2,1,0:T(2,128)(2,1)S(1)} %broadcast_select_fusion), kind=kLoop, calls=%fused_computation.17 | loop fusion | flops 1081344 | bytes 4325376 | tf_op jit(solution)/shard_map/concatenate | solution.py:129
  330.4 25.8 %reduce-scatter.2.cloned.1.call-done = bf16[16,256]{1,0:T(8,128)(2,1)} async-done(((bf16[16,2048]{1,0:T(8,128)(2,1)}), bf16[16,256]{1,0:T(8,128)(2,1)}) %reduce-scatter.2.cloned.1.call-update) | async-done | bytes 8208 | tf_op jit(solution)/shard_map/reduce_scatter | solution.py:156
  356.3 1.3 add_convert_fusion
  (77 shorter events, 9.6 us)
Async XLA Ops:
  7.2 312.7 %copy-start = (bf16[256,2048]{1,0:T(8,128)(2,1)S(1)}, bf16[256,2048]{1,0:T(8,128)(2,1)}, u32[]{:S(2)}) copy-start(bf16[256,2048]{1,0:T(8,128)(2,1)} %param.12) | copy-start | bytes 3145732
  49.5 12.4 %copy-start.1 = (s32[512]{0:T(512)S(1)}, s32[512]{0:T(512)}, u32[]{:S(2)}) copy-start(s32[512]{0:T(512)} %param.15) | copy-start | bytes 6148
  49.5 14.8 %copy-start.2 = (s32[512]{0:T(512)S(1)}, s32[512]{0:T(512)}, u32[]{:S(2)}) copy-start(s32[512]{0:T(512)} %param.17) | copy-start | bytes 6148
  49.5 17.3 %copy-start.3 = (s32[512]{0:T(512)S(1)}, s32[512]{0:T(512)}, u32[]{:S(2)}) copy-start(s32[512]{0:T(512)} %param.16) | copy-start | bytes 6148
  49.5 200.5 %all-to-all-start = ((bf16[32,256,512]{2,1,0:T(8,128)(2,1)}), bf16[32,256,512]{2,1,0:T(8,128)(2,1)}, u32[]{:S(2)}, u32[]{:S(2)}) async-start(bf16[32,256,512]{2,1,0:T(8,128)(2,1)} %reshape.445), calls=%async_computation | async-start | bytes 16777216 | tf_op jit(solution)/shard_map/all_to_all | solution.py:117
  61.8 294.5 %reduce-scatter.2.cloned.1.call-start = ((), (), s32[]{:S(2)}) async-start(), calls=%async_computation.2 | async-start | bytes 73728 | tf_op jit(solution)/shard_map/reduce_scatter | solution.py:156
  67.4 6.7 %copy-start.5 = (bf16[16,256]{1,0:T(8,128)(2,1)S(1)}, bf16[16,256]{1,0:T(8,128)(2,1)}, u32[]{:S(2)}) copy-start(bf16[16,256]{1,0:T(8,128)(2,1)} %param.10) | copy-start | bytes 24580
  315.6 5.2 %copy-start.4 = (bf16[16,128,2,256]{3,2,1,0:T(2,128)(2,1)S(1)}, bf16[16,128,2,256]{3,2,1,0:T(2,128)(2,1)}, u32[]{:S(2)}) copy-start(bf16[16,128,2,256]{3,2,1,0:T(2,128)(2,1)} %gather.56) | copy-start | bytes 6291460
Sparse Core Ops, SparseCore 0:
  320.9 35.3 reduce-scatter.1
where the time goes:
time: 368 us; the launch traced here: 364 us
  waiting for transfers between devices  184 us (50%)
  local copies, waits for them, and re-layouts  111 us (30%)
  other arithmetic  17.2 us (5%)
  between operations  14.3 us (4%)
  blocking collectives  14.1 us (4%)
  starting transfers between devices  12.3 us (3%)
  matrix products  12.1 us (3%)
    all_to_all x1, waiting for transfers between devices, local(): lax.all_to_all(outgoing_pages, 'blk', split_axis=0, concat_axis=0, tiled=...  158 us
    gather x2, local copies, waits for them, and re-layouts, local(): kept_rows = arrived[receive_slots[:, None], landed_keep]  55.3 us
    reduce_scatter x1, waiting for transfers between devices, local(): lax.psum_scatter(partial_value.astype(jnp.bfloat16), 'head', scatter_dime...  25.8 us
    gather x1, local copies, waits for them, and re-layouts, local(): cache_pool[slot_pages].reshape(buffer_rows, -1, 2 * head_width)  21.8 us
    all_gather x1, blocking collectives, local(): gathered = lax.all_gather(hidden_in, 'head', axis=1, tiled=True)  14.1 us
    reshape x1, local copies, waits for them, and re-layouts, local(): cache_pool[slot_pages].reshape(buffer_rows, -1, 2 * head_width)  14 us
    all_to_all x1, starting transfers between devices, local(): lax.all_to_all(outgoing_pages, 'blk', split_axis=0, concat_axis=0, tiled=...  12.3 us
    select_n x2, other arithmetic, local(): jnp.where(landed_layout[3][:, :, None], kept_rows, jnp.zeros((), jnp.bflo...  8.09 us
  transfers between devices with their start and end apart: 2, of which 2 were waited for; matrix products, arithmetic and copies ran while one was open for 7% of the time, Pallas kernels for 0%

commit v1 on v0

v1 whole, which is shorter than its diff:
```python
import jax
import jax.numpy as jnp
from jax import lax
from jax.experimental import pallas as pl
from jax.experimental.pallas import tpu as pltpu
from jax.sharding import PartitionSpec as P

HEAD_DIM = 128
PAGE = 64
PAGES = 4
CAP = 256
KEPT = 128
SLOTS = 132
HEADS_HERE = 2
LANES = HEADS_HERE * 2
ROWS = SLOTS * LANES
PAD_ROWS = 640
NEG = -1e30

epsilon = 1e-05


def layer_norm(hidden):
    average = jnp.mean(hidden, axis=-1, keepdims=True)
    centered = hidden - average
    variance = jnp.mean(centered * centered, axis=-1, keepdims=True)
    return centered * lax.rsqrt(variance + epsilon)


def rotate(vectors, positions):
    half_dim = vectors.shape[-1] // 2
    inverse_freq = 10000.0 ** (-jnp.arange(half_dim, dtype=jnp.float32) / half_dim)
    angles = positions.astype(jnp.float32)[:, None, None] * inverse_freq
    cosine = jnp.cos(angles)
    sine_part = jnp.sin(angles)
    first_half = vectors[..., :half_dim]
    second_half = vectors[..., half_dim:]
    return jnp.concatenate(
        [
            first_half * cosine - second_half * sine_part,
            second_half * cosine + first_half * sine_part,
        ],
        axis=-1,
    )


def pack_kernel(
    target_ref,
    page_ref,
    keep_smem,
    keep_ref,
    length_ref,
    weight_ref,
    cache_rows_hbm,
    cache_flat_hbm,
    send_hbm,
    rows_vmem,
    flat_vmem,
    out_vmem,
    wide_vmem,
    in_sem,
    flat_sem,
    out_sem,
):
    count = keep_ref.shape[0]

    def page_copies(i):
        copies = []
        for j in range(PAGES):
            page = page_ref[j, i]
            copies.append(
                pltpu.make_async_copy(
                    cache_rows_hbm.at[page],
                    rows_vmem.at[i, pl.ds(j * PAGE, PAGE)],
                    in_sem.at[i, j],
                )
            )
            copies.append(
                pltpu.make_async_copy(
                    cache_flat_hbm.at[page],
                    flat_vmem.at[i, pl.ds(j * PAGE * LANES, PAGE * LANES)],
                    flat_sem.at[i, j],
                )
            )
        return copies

    def start(i, carry):
        for copy in page_copies(i):
            copy.start()
        return carry

    lax.fori_loop(0, count, start, 0)

    keep_cols = jnp.transpose(keep_ref[...].astype(jnp.float32))
    lane_pos = lax.broadcasted_iota(jnp.int32, (KEPT, CAP), 1).astype(jnp.float32)
    kept_rows = []
    for i in range(count):
        match = keep_cols[:, i : i + 1] == lane_pos
        kept_rows.append(jnp.max(jnp.where(match, 1.0, 0.0), axis=0, keepdims=True))
    kept = jnp.concatenate(kept_rows, axis=0)
    spots = lax.broadcasted_iota(jnp.int32, (count, CAP), 1)
    dropped = (spots < length_ref[...]) & (kept < 0.5)
    factors = jnp.where(dropped, weight_ref[...], 0.0).astype(jnp.bfloat16)
    spread = (
        lax.broadcasted_iota(jnp.int32, (CAP, CAP * LANES), 1) // LANES
        == lax.broadcasted_iota(jnp.int32, (CAP, CAP * LANES), 0)
    )
    spread = jnp.where(spread, 1.0, 0.0).astype(jnp.bfloat16)
    wide_vmem[...] = jnp.dot(factors, spread, preferred_element_type=jnp.float32)
    row_id = lax.broadcasted_iota(jnp.int32, (PAGES * LANES, CAP * LANES), 0)
    lane_id = lax.broadcasted_iota(jnp.int32, (PAGES * LANES, CAP * LANES), 1)
    selector = (row_id // LANES == lane_id // (PAGE * LANES)) & (row_id % LANES == lane_id % LANES)
    selector = jnp.where(selector, 1.0, 0.0)
    zero_row = jnp.zeros((1, LANES, HEAD_DIM), jnp.bfloat16)

    def out_copy(i):
        return pltpu.make_async_copy(out_vmem.at[i], send_hbm.at[target_ref[i]], out_sem.at[i])

    def body(i, carry):
        for copy in page_copies(i):
            copy.wait()
        rows_vmem[i, pl.ds(CAP, 1)] = zero_row
        left = (selector * wide_vmem[pl.ds(i, 1), :]).astype(jnp.bfloat16)
        merged = jnp.dot(left, flat_vmem[i], preferred_element_type=jnp.float32)
        out_vmem[i, pl.ds(KEPT, PAGES)] = merged.astype(jnp.bfloat16).reshape(
            PAGES, LANES, HEAD_DIM
        )

        def chunk(c, inner):
            for u in range(16):
                s = c * 16 + u
                out_vmem[i, s] = rows_vmem[i, keep_smem[i, s]]
            return inner

        lax.fori_loop(0, KEPT // 16, chunk, 0)
        out_copy(i).start()
        return carry

    lax.fori_loop(0, count, body, 0)

    def finish(i, carry):
        out_copy(i).wait()
        return carry

    lax.fori_loop(0, count, finish, 0)


def pack(targets, pages, keep, lengths, weights, cache_pool, buffers):
    count = keep.shape[0]
    pool = cache_pool.shape[0]
    view = cache_pool.reshape(pool, PAGE, 2, HEADS_HERE, HEAD_DIM).transpose(0, 1, 3, 2, 4)
    as_rows = view.reshape(pool, PAGE, LANES, HEAD_DIM)
    as_flat = view.reshape(pool, PAGE * LANES, HEAD_DIM)
    whole = lambda: pl.BlockSpec(memory_space=pltpu.VMEM)
    hbm = lambda: pl.BlockSpec(memory_space=pl.ANY)
    return pl.pallas_call(
        pack_kernel,
        out_shape=jax.ShapeDtypeStruct((buffers, SLOTS, LANES, HEAD_DIM), jnp.bfloat16),
        grid_spec=pltpu.PrefetchScalarGridSpec(
            num_scalar_prefetch=3,
            grid=(),
            in_specs=[whole(), whole(), whole(), hbm(), hbm()],
            out_specs=hbm(),
            scratch_shapes=[
                pltpu.VMEM((count, CAP + 1, LANES, HEAD_DIM), jnp.bfloat16),
                pltpu.VMEM((count, CAP * LANES, HEAD_DIM), jnp.bfloat16),
                pltpu.VMEM((count, SLOTS, LANES, HEAD_DIM), jnp.bfloat16),
                pltpu.VMEM((count, CAP * LANES), jnp.float32),
                pltpu.SemaphoreType.DMA((count, PAGES)),
                pltpu.SemaphoreType.DMA((count, PAGES)),
                pltpu.SemaphoreType.DMA((count,)),
            ],
        ),
        compiler_params=pltpu.CompilerParams(vmem_limit_bytes=40 * 1024 * 1024),
        name="pack",
    )(targets, pages, keep, keep, lengths, weights, as_rows, as_flat)


def attend_kernel(
    source_ref,
    query_ref,
    key_ref,
    value_ref,
    bias_ref,
    weight_ref,
    recv_hbm,
    packed_hbm,
    share_ref,
    rows_vmem,
    attended_vmem,
    in_sem,
    out_sem,
):
    count = query_ref.shape[0]

    def in_copy(r):
        return pltpu.make_async_copy(
            recv_hbm.at[source_ref[r]], rows_vmem.at[r, pl.ds(0, ROWS)], in_sem.at[r]
        )

    def out_copy(r):
        return pltpu.make_async_copy(
            rows_vmem.at[r, pl.ds(0, ROWS)], packed_hbm.at[r], out_sem.at[r]
        )

    for r in range(count):
        in_copy(r).start()
    for r in range(count):
        rows_vmem[r, pl.ds(ROWS, PAD_ROWS - ROWS)] = jnp.zeros(
            (PAD_ROWS - ROWS, HEAD_DIM), jnp.bfloat16
        )
    scale = HEAD_DIM ** (-0.5)
    contract_last = (((1,), (1,)), ((), ()))
    own = (
        jnp.sum(
            query_ref[...].astype(jnp.float32) * key_ref[...].astype(jnp.float32),
            axis=-1,
            keepdims=True,
        )
        * scale
    )
    for r in range(count):
        in_copy(r).wait()
        out_copy(r).start()
        scores = lax.dot_general(
            query_ref[r], rows_vmem[r], contract_last, preferred_element_type=jnp.float32
        )
        scores = scores * scale + bias_ref[r]
        own_score = own[r]
        highest = jnp.maximum(jnp.max(scores, axis=-1, keepdims=True), own_score)
        exponentials = jnp.exp(scores - highest)
        own_exp = jnp.exp(own_score - highest)
        denominator = jnp.sum(exponentials, axis=-1, keepdims=True) + own_exp
        probabilities = exponentials / denominator
        own_prob = (own_exp / denominator).astype(jnp.bfloat16).astype(jnp.float32)
        moved = pltpu.roll(probabilities, 1, axis=1).astype(jnp.bfloat16)
        combined = jnp.dot(moved, rows_vmem[r], preferred_element_type=jnp.float32)
        combined = combined + own_prob * value_ref[r].astype(jnp.float32)
        attended_vmem[r] = combined
    attended = jnp.concatenate(
        [attended_vmem[:, h, :] for h in range(HEADS_HERE)], axis=1
    ).astype(jnp.bfloat16)
    share = jnp.dot(attended, weight_ref[...], preferred_element_type=jnp.float32).astype(
        jnp.bfloat16
    )
    peers = share_ref.shape[0]
    width = share_ref.shape[2]
    for e in range(peers):
        share_ref[e] = share[:, e * width : (e + 1) * width]
    for r in range(count):
        out_copy(r).wait()


def attend(sources, queries, keys, values, bias, out_weight, recv, peers):
    count = queries.shape[0]
    width = out_weight.shape[1] // peers
    whole = lambda: pl.BlockSpec(memory_space=pltpu.VMEM)
    hbm = lambda: pl.BlockSpec(memory_space=pl.ANY)
    return pl.pallas_call(
        attend_kernel,
        out_shape=(
            jax.ShapeDtypeStruct((count, ROWS, HEAD_DIM), jnp.bfloat16),
            jax.ShapeDtypeStruct((peers, count, width), jnp.bfloat16),
        ),
        grid_spec=pltpu.PrefetchScalarGridSpec(
            num_scalar_prefetch=1,
            grid=(),
            in_specs=[whole(), whole(), whole(), whole(), whole(), hbm()],
            out_specs=[hbm(), whole()],
            scratch_shapes=[
                pltpu.VMEM((count, PAD_ROWS, HEAD_DIM), jnp.bfloat16),
                pltpu.VMEM((count, 8, HEAD_DIM), jnp.float32),
                pltpu.SemaphoreType.DMA((count,)),
                pltpu.SemaphoreType.DMA((count,)),
            ],
        ),
        compiler_params=pltpu.CompilerParams(vmem_limit_bytes=32 * 1024 * 1024),
        name="attend",
    )(sources, queries, keys, values, bias, out_weight, recv)


def local(
    hidden_in,
    qkv_weight,
    out_weight,
    cache_pool,
    page_table,
    request_order,
    request_lengths,
    retained_counts,
    retained_positions,
    blended_weight,
):
    rows_here = hidden_in.shape[0]
    head_width = qkv_weight.shape[2]
    heads_here = head_width // HEAD_DIM
    blocks = lax.axis_size("blk")
    peers = lax.axis_size("head")
    block_index = lax.axis_index("blk")
    first = block_index * rows_here
    local_slots = jnp.arange(rows_here, dtype=jnp.int32)
    slot_index = jnp.arange(KEPT, dtype=jnp.int32)
    own_ids = first + local_slots

    places = jnp.arange(request_order.shape[0], dtype=jnp.int32) // rows_here
    targets = jnp.sum(
        jnp.where(request_order[None, :] == own_ids[:, None], places[None, :], 0), axis=1
    )
    take = lambda array: lax.dynamic_slice_in_dim(array, first, rows_here, 0)
    own_counts = take(retained_counts)
    own_keep = jnp.where(
        slot_index[None, :] < own_counts[:, None], take(retained_positions), CAP
    )
    outgoing = pack(
        targets,
        page_table.T,
        own_keep,
        take(request_lengths)[:, None],
        take(blended_weight),
        cache_pool,
        blocks,
    )
    outgoing = outgoing.reshape(blocks, ROWS, HEAD_DIM)
    arrived = lax.all_to_all(outgoing, "blk", split_axis=0, concat_axis=0, tiled=True)

    old_ids = take(request_order)
    sources = old_ids // rows_here
    lengths = request_lengths[old_ids]
    counts = retained_counts[old_ids]
    keep = jnp.where(slot_index[None, :] < counts[:, None], retained_positions[old_ids], CAP)
    spots = jnp.arange(CAP, dtype=jnp.int32)
    dropped = (spots[None, :] < lengths[:, None]) & jnp.logical_not(
        jnp.any(keep[:, :, None] == spots[None, None, :], axis=1)
    )
    dropped_weight = jnp.where(dropped, blended_weight[old_ids], 0.0)
    dropped_mass = jnp.log(1.0 + jnp.sum(dropped_weight.reshape(rows_here, PAGES, PAGE), axis=2))
    page_start = jnp.arange(PAGES, dtype=jnp.int32) * PAGE
    bias_slots = jnp.concatenate(
        [
            jnp.where(slot_index[None, :] < counts[:, None], 0.0, NEG),
            jnp.where(page_start[None, :] < lengths[:, None], dropped_mass, NEG),
        ],
        axis=1,
    )
    columns = jnp.arange(ROWS, dtype=jnp.int32) % LANES
    head_rows = jnp.arange(8, dtype=jnp.int32)
    bias = jnp.where(
        columns[None, None, :] == 2 * head_rows[None, :, None],
        jnp.repeat(bias_slots, LANES, axis=1)[:, None, :],
        NEG,
    )
    bias = jnp.pad(bias, ((0, 0), (0, 0), (0, PAD_ROWS - ROWS)), constant_values=NEG)

    gathered = lax.all_gather(hidden_in, "head", axis=1, tiled=True)
    normed = layer_norm(gathered.astype(jnp.float32)).astype(jnp.bfloat16)
    project = lambda index: jnp.dot(
        normed, qkv_weight[:, index], preferred_element_type=jnp.float32
    ).reshape(rows_here, heads_here, HEAD_DIM)
    pad_heads = lambda array: jnp.pad(
        array.astype(jnp.bfloat16), ((0, 0), (0, 8 - heads_here), (0, 0))
    )
    queries = pad_heads(rotate(project(0), lengths))
    new_keys = pad_heads(rotate(project(1), lengths))
    new_values = pad_heads(project(2))

    packed, share = attend(
        sources, queries, new_keys, new_values, bias, out_weight, arrived, peers
    )
    parts = lax.all_to_all(share, "head", split_axis=0, concat_axis=0, tiled=True)
    summed = jnp.sum(parts.astype(jnp.float32), axis=0)
    hidden_out = (hidden_in.astype(jnp.float32) + summed).astype(jnp.bfloat16)
    packed_cache = (
        packed.reshape(rows_here, SLOTS, heads_here, 2, HEAD_DIM)
        .transpose(0, 1, 3, 2, 4)
        .reshape(rows_here, SLOTS, 2, head_width)
    )
    return (hidden_out, packed_cache)


def solution(mesh):
    return jax.shard_map(
        local,
        mesh=mesh,
        in_specs=(
            P("blk", "head"),
            P(None, None, "head"),
            P("head", None),
            P("blk", None, None, "head"),
            P("blk", None),
            P(),
            P(),
            P(),
            P(),
            P(),
        ),
        out_specs=(P("blk", "head"), P("blk", None, None, "head")),
        check_vma=False,
    )
```

time: 368 us -> 169 us (0.46)
  waiting for transfers between devices: 184 us -> 64.7 us
  local copies, waits for them, and re-layouts: 111 us -> 18.6 us
  Pallas kernels: 0 us -> 36.3 us
  blocking collectives: 14.1 us -> 28.2 us
  between operations: 14.3 us -> 0.87 us
  other arithmetic: 17.2 us -> 4.61 us
  matrix products: 12.1 us -> 2.37 us
    all_to_all x1, waiting for transfers between devices: 158 us -> 64.7 us  [local(): lax.all_to_all(outgoing, 'blk', split_axis=0, concat_axis=0, tiled=True)]
    gather x13 -> x5, local copies, waits for them, and re-layouts: 84.2 us -> 3.51 us  [the longest x1 1.52 us: local(): retained_positions[old_ids]]
    pallas_call x0 -> x2, Pallas kernels: none -> 36.3 us  [the longest x1 25.2 us: pack(): pl.pallas_call(pack_kernel, out_shape=jax.ShapeDtypeStruct((buffers, SLOT...]
    reduce_scatter x1 -> x0, waiting for transfers between devices: 25.8 us -> none  [local(): lax.psum_scatter(partial_value.astype(jnp.bfloat16), 'head', scatter_dime...]
    reshape x3 -> x0, local copies, waits for them, and re-layouts: 16.3 us -> none  [the longest x1 14 us: local(): cache_pool[slot_pages].reshape(buffer_rows, -1, 2 * head_width)]
    all_to_all x0 -> x1, blocking collectives: none -> 14.4 us  [local(): lax.all_to_all(share, 'head', split_axis=0, concat_axis=0, tiled=True)]
    dot_general x5 -> x3, matrix products: 12.1 us -> 2.37 us  [local(): jnp.dot(normed, qkv_weight[:, index], preferred_element_type=jnp.float32)]
    dot_general x0 -> x5, local copies, waits for them, and re-layouts: none -> 8 us  [local(): jnp.dot(normed, qkv_weight[:, index], preferred_element_type=jnp.float32)]
  transfers between devices with their start and end apart: 2 -> 1, of which waited for: 2 -> 1; matrix products, arithmetic and copies ran while one was open for 7% -> 10% of each run, Pallas kernels for 0% -> 0%
where the time goes in v1:
time: 169 us; the launch traced here: 168 us
  waiting for transfers between devices  64.7 us (38%)
  Pallas kernels  36.3 us (21%)
  blocking collectives  28.2 us (17%)
  local copies, waits for them, and re-layouts  18.6 us (11%)
  starting transfers between devices  12.3 us (7%)
  other arithmetic  4.61 us (3%)
  matrix products  2.37 us (1%)
    all_to_all x1, waiting for transfers between devices, local(): lax.all_to_all(outgoing, 'blk', split_axis=0, concat_axis=0, tiled=True)  64.7 us
    pallas_call x1, Pallas kernels, pack(): pl.pallas_call(pack_kernel, out_shape=jax.ShapeDtypeStruct((buffers, SLOT...  25.2 us
    all_to_all x1, blocking collectives, local(): lax.all_to_all(share, 'head', split_axis=0, concat_axis=0, tiled=True)  14.4 us
    all_gather x1, blocking collectives, local(): gathered = lax.all_gather(hidden_in, 'head', axis=1, tiled=True)  13.9 us
    all_to_all x1, starting transfers between devices, local(): lax.all_to_all(outgoing, 'blk', split_axis=0, concat_axis=0, tiled=True)  12.3 us
    pallas_call x1, Pallas kernels, attend(): pl.pallas_call(attend_kernel, out_shape=(jax.ShapeDtypeStruct((count, ROW...  11 us
    dot_general x5, local copies, waits for them, and re-layouts, local(): jnp.dot(normed, qkv_weight[:, index], preferred_element_type=jnp.float32)  8 us
    unnamed x16, local copies, waits for them, and re-layouts  4.91 us
  transfers between devices with their start and end apart: 1, of which 1 were waited for; matrix products, arithmetic and copies ran while one was open for 10% of the time, Pallas kernels for 0%

profile of v1, /device:TPU:1, one launch (start us, length us, event | category | flops | bytes accessed | tf_op | source)
XLA Modules:
  0.0 168.0 jit_solution(6999303387967917332)
XLA Ops:
  0.7 0.8 dynamic-slice_bitcast_fusion
  1.5 0.8 dynamic_slice.16
  2.3 0.8 dynamic-slice_select_fusion.keep_smem.keep_ref
  3.1 0.9 select_reduce_fusion.target_ref
  4.0 2.2 %copy-done.2 = bf16[64,64,2,256]{3,2,1,0:T(2,128)(2,1)S(1)} copy-done((bf16[64,64,2,256]{3,2,1,0:T(2,128)(2,1)S(1)}, bf16[64,64,2,256]{3,2,1,0:T(2,128)(2,1)}, u32[]{:S(2)}) %copy-start.2) | copy-done | bytes 4194328
  6.2 0.7 copy-done.4
  6.8 25.2 %pack.1 = bf16[32,132,4,128]{3,2,1,0:T(4,128)(2,1)S(1)} custom-call(s32[16]{0:T(128)S(1)} %select_reduce_fusion.target_ref, s32[4,16]{1,0:T(4,128)S(1)} %bitcast.43, s32[16,128]{1,0:T(8,128)S(1)} %dynamic-slice_select_fusion.keep_smem.keep_ref, s32[16,128]{1,0:T(8,128)S(1)} %dynamic-slice_select_fusion.keep_smem.keep_ref, s32[16,1]{1,0:T(8,128)S(1)} %copy.47.length_ref, ...), custom_call_target="tpu_custom_call" | custom-call | tf_op jit(solution)/shard_map/pack/pallas_call | solution.py:156
  32.1 2.0 %copy-done.1 = bf16[32,132,4,128]{3,2,1,0:T(4,128)(2,1)} copy-done((bf16[32,132,4,128]{3,2,1,0:T(4,128)(2,1)}, bf16[32,132,4,128]{3,2,1,0:T(4,128)(2,1)S(1)}, u32[]{:S(2)}) %copy-start.1) | copy-done | bytes 4325400
  34.1 12.3 %all-to-all-start = ((bf16[32,528,128]{2,1,0:T(8,128)(2,1)}), bf16[32,528,128]{2,1,0:T(8,128)(2,1)}, u32[]{:S(2)}, u32[]{:S(2)}) async-start(bf16[32,528,128]{2,1,0:T(8,128)(2,1)} %bitcast.40), calls=%async_computation | async-start | bytes 8650752 | tf_op jit(solution)/shard_map/all_to_all | solution.py:324
  46.4 0.8 compare_select_fusion
  47.2 0.7 gather_fusion
  47.9 0.7 gather_fusion.1
  48.5 1.5 gather_fusion.2
  50.0 0.6 gather_fusion.3
  51.9 3.5 %slice_bitcast_fusion = (bf16[256,2048]{0,1:T(8,128)(2,1)}, bf16[256,2048]{0,1:T(8,128)(2,1)S(1)}, bf16[256,2048]{0,1:T(8,128)(2,1)}) fusion(bf16[2048,3,256]{2,0,1:T(8,128)(2,1)} %param.11), kind=kLoop, calls=%fused_computation.6 | loop fusion | bytes 6291456 | tf_op jit(solution)/shard_map/dot_general | solution.py:356
  55.4 1.5 copy.42
  56.9 13.9 %all_gather.3 = bf16[16,2048]{1,0:T(8,128)(2,1)S(1)} all-gather(bf16[16,256]{1,0:T(8,128)(2,1)S(1)} %copy-done.7), channel_id=1, replica_groups=mesh['head'=8,'blk'=32] {'head'}, dimensions={1}, use_global_device_ids=true | all-gather | bytes 73728 | tf_op jit(solution)/shard_map/all_gather | solution.py:354
  71.6 1.4 copy.36
  73.0 1.6 copy.39
  74.9 1.6 fusion.21
  77.2 64.7 %all-to-all-done.recv_hbm = bf16[32,528,128]{2,1,0:T(8,128)(2,1)} async-done(((bf16[32,528,128]{2,1,0:T(8,128)(2,1)}), bf16[32,528,128]{2,1,0:T(8,128)(2,1)}, u32[]{:S(2)}, u32[]{:S(2)}) %all-to-all-start) | async-done | bytes 4325408 | tf_op jit(solution)/shard_map/all_to_all | solution.py:324
  142.0 11.0 %attend.1 = (bf16[16,528,128]{2,1,0:T(8,128)(2,1)}, bf16[8,16,256]{2,1,0:T(8,128)(2,1)S(1)}) custom-call(s32[16]{0:T(128)S(1)} %get-tuple-element.20.source_ref, bf16[16,8,128]{2,1,0:T(8,128)(2,1)S(1)} %get-tuple-element.23.query_ref, bf16[16,8,128]{2,1,0:T(8,128)(2,1)S(1)} %get-tuple-element.24.key_ref, bf16[16,8,128]{2,1,0:T(8,128)(2,1)S(1)} %pad.16.value_ref, ...), custom_call_target="tpu_custom_call" | custom-call | tf_op jit(solution)/shard_map/attend/pallas_call | solution.py:259
  153.0 14.4 %all_to_all.10 = bf16[8,16,256]{2,1,0:T(8,128)(2,1)S(1)} all-to-all(bf16[8,16,256]{2,1,0:T(8,128)(2,1)S(1)} %get-tuple-element.4), channel_id=1, replica_groups=mesh['head'=8,'blk'=32] {'head'}, dimensions={0} | all-to-all | bytes 131072 | tf_op jit(solution)/shard_map/all_to_all | solution.py:369
  167.4 0.6 add_convert_fusion
  (53 shorter events, 3.1 us)
Async XLA Ops:
  0.6 1.7 %copy-start = (f32[512,256]{1,0:T(8,128)S(1)}, f32[512,256]{1,0:T(8,128)}, u32[]{:S(2)}) copy-start(f32[512,256]{1,0:T(8,128)} %param.19) | copy-start | bytes 1572868
  4.0 2.2 %copy-start.2 = (bf16[64,64,2,256]{3,2,1,0:T(2,128)(2,1)S(1)}, bf16[64,64,2,256]{3,2,1,0:T(2,128)(2,1)}, u32[]{:S(2)}) copy-start(bf16[64,64,2,256]{3,2,1,0:T(2,128)(2,1)} %param.13) | copy-start | bytes 12582916
  6.2 0.7 copy-start.4
  32.1 2.0 %copy-start.1 = (bf16[32,132,4,128]{3,2,1,0:T(4,128)(2,1)}, bf16[32,132,4,128]{3,2,1,0:T(4,128)(2,1)S(1)}, u32[]{:S(2)}) copy-start(bf16[32,132,4,128]{3,2,1,0:T(4,128)(2,1)S(1)} %pack.1) | copy-start | bytes 12976132
  34.1 13.1 %copy-start.5 = (s32[512]{0:T(512)S(1)}, s32[512]{0:T(512)}, u32[]{:S(2)}) copy-start(s32[512]{0:T(512)} %param.16) | copy-start | bytes 6148
  34.1 13.7 %copy-start.6 = (s32[512]{0:T(512)S(1)}, s32[512]{0:T(512)}, u32[]{:S(2)}) copy-start(s32[512]{0:T(512)} %param.17) | copy-start | bytes 6148
  34.1 107.8 %all-to-all-start = ((bf16[32,528,128]{2,1,0:T(8,128)(2,1)}), bf16[32,528,128]{2,1,0:T(8,128)(2,1)}, u32[]{:S(2)}, u32[]{:S(2)}) async-start(bf16[32,528,128]{2,1,0:T(8,128)(2,1)} %bitcast.40), calls=%async_computation | async-start | bytes 8650752 | tf_op jit(solution)/shard_map/all_to_all | solution.py:324
  51.9 5.0 %copy-start.7 = (bf16[16,256]{1,0:T(8,128)(2,1)S(1)}, bf16[16,256]{1,0:T(8,128)(2,1)}, u32[]{:S(2)}) copy-start(bf16[16,256]{1,0:T(8,128)(2,1)} %param.10) | copy-start | bytes 24580
  73.0 69.0 %copy-start.3 = (bf16[256,2048]{1,0:T(8,128)(2,1)S(1)}, bf16[256,2048]{1,0:T(8,128)(2,1)}, u32[]{:S(2)}) copy-start(bf16[256,2048]{1,0:T(8,128)(2,1)} %weight_ref.1) | copy-start | bytes 3145732

commit v2 on v1

v2 whole, which is shorter than its diff:
```python
import jax
import jax.numpy as jnp
from jax import lax
from jax.experimental import pallas as pl
from jax.experimental.pallas import tpu as pltpu
from jax.sharding import PartitionSpec as P

HEAD_DIM = 128
PAGE = 64
PAGES = 4
CAP = 256
KEPT = 128
SLOTS = 132
HEADS_HERE = 2
LANES = HEADS_HERE * 2
ROWS = SLOTS * LANES
PAD_ROWS = 640
NEG = -1e30

epsilon = 1e-05


def layer_norm(hidden):
    average = jnp.mean(hidden, axis=-1, keepdims=True)
    centered = hidden - average
    variance = jnp.mean(centered * centered, axis=-1, keepdims=True)
    return centered * lax.rsqrt(variance + epsilon)


def rotate(vectors, positions):
    half_dim = vectors.shape[-1] // 2
    inverse_freq = 10000.0 ** (-jnp.arange(half_dim, dtype=jnp.float32) / half_dim)
    angles = positions.astype(jnp.float32)[:, None, None] * inverse_freq
    cosine = jnp.cos(angles)
    sine_part = jnp.sin(angles)
    first_half = vectors[..., :half_dim]
    second_half = vectors[..., half_dim:]
    return jnp.concatenate(
        [
            first_half * cosine - second_half * sine_part,
            second_half * cosine + first_half * sine_part,
        ],
        axis=-1,
    )


def pack_kernel(
    block_ref,
    page_hbm,
    length_hbm,
    count_hbm,
    order_hbm,
    keep_hbm,
    weight_hbm,
    cache_rows_hbm,
    cache_flat_hbm,
    send_hbm,
    rows_vmem,
    flat_vmem,
    out_vmem,
    wide_vmem,
    order_vmem,
    keep_vmem,
    weight_vmem,
    spot_vmem,
    page_smem,
    length_smem,
    count_smem,
    spot_smem,
    small_sem,
    load_sem,
    spot_sem,
    out_sem,
):
    count = keep_vmem.shape[0]
    pool_rows = cache_rows_hbm.shape[0]
    first = pl.multiple_of(block_ref[0] * count, count)
    small = [
        pltpu.make_async_copy(source, target, small_sem.at[n])
        for n, (source, target) in enumerate(
            [
                (keep_hbm.at[pl.ds(first, count)], keep_vmem),
                (count_hbm, count_smem),
                (page_hbm, page_smem),
                (order_hbm, order_vmem),
                (length_hbm, length_smem),
                (weight_hbm.at[pl.ds(first, count)], weight_vmem),
            ]
        )
    ]
    for copy in small:
        copy.start()
    load_rows = pltpu.make_async_copy(
        cache_rows_hbm, rows_vmem.at[pl.ds(0, pool_rows)], load_sem.at[0]
    )
    load_flat = pltpu.make_async_copy(cache_flat_hbm, flat_vmem, load_sem.at[1])
    load_rows.start()
    load_flat.start()
    for copy in small:
        copy.wait()

    keep = keep_vmem[...]
    slot_id = lax.broadcasted_iota(jnp.int32, keep.shape, 1)
    row_id = lax.broadcasted_iota(jnp.int32, keep.shape, 0)
    counts = jnp.zeros(keep.shape, jnp.int32)
    base = jnp.zeros(keep.shape, jnp.int32)
    page_of = keep >> 6
    for i in range(count):
        here = row_id == i
        counts = jnp.where(here, count_smem[first + i], counts)
        for j in range(PAGES):
            base = jnp.where(here & (page_of == j), page_smem[j, i] * PAGE, base)
    keep = jnp.where(slot_id < counts, keep, CAP)
    spot_vmem[...] = jnp.where(slot_id < counts, base + (keep & (PAGE - 1)), pool_rows)
    move_spots = pltpu.make_async_copy(spot_vmem, spot_smem, spot_sem)
    move_spots.start()

    order = order_vmem[...]
    place = (
        lax.broadcasted_iota(jnp.int32, order.shape, 0) * order.shape[1]
        + lax.broadcasted_iota(jnp.int32, order.shape, 1)
    ) // count
    targets = [jnp.sum(jnp.where(order == first + i, place, 0)) for i in range(count)]

    keep_cols = jnp.transpose(keep.astype(jnp.float32))
    lane_pos = lax.broadcasted_iota(jnp.int32, (KEPT, CAP), 1).astype(jnp.float32)
    spot = lax.broadcasted_iota(jnp.int32, (1, CAP), 1)
    factors = []
    for i in range(count):
        match = keep_cols[:, i : i + 1] == lane_pos
        kept = jnp.max(jnp.where(match, 1.0, 0.0), axis=0, keepdims=True)
        dropped = (spot < length_smem[first + i]) & (kept < 0.5)
        factors.append(jnp.where(dropped, weight_vmem[i : i + 1, :], 0.0))
    factors = jnp.concatenate(factors, axis=0).astype(jnp.bfloat16)
    spread = (
        lax.broadcasted_iota(jnp.int32, (CAP, CAP * LANES), 1) >> 2
        == lax.broadcasted_iota(jnp.int32, (CAP, CAP * LANES), 0)
    )
    spread = jnp.where(spread, 1.0, 0.0).astype(jnp.bfloat16)
    wide_vmem[...] = jnp.dot(factors, spread, preferred_element_type=jnp.float32)
    page_lanes = PAGE * LANES
    out_row = lax.broadcasted_iota(jnp.int32, (PAGES * LANES, page_lanes), 0)
    out_lane = lax.broadcasted_iota(jnp.int32, (PAGES * LANES, page_lanes), 1)
    same = (out_row & (LANES - 1)) == (out_lane & (LANES - 1))
    selectors = [jnp.where(same & (out_row >> 2 == j), 1.0, 0.0) for j in range(PAGES)]

    load_flat.wait()
    for i in range(count):
        merged = jnp.zeros((PAGES * LANES, HEAD_DIM), jnp.float32)
        for j in range(PAGES):
            wide = wide_vmem[i : i + 1, j * page_lanes : (j + 1) * page_lanes]
            merged = merged + jnp.dot(
                (selectors[j] * wide).astype(jnp.bfloat16),
                flat_vmem[page_smem[j, i]],
                preferred_element_type=jnp.float32,
            )
        out_vmem[i, pl.ds(KEPT, PAGES)] = merged.astype(jnp.bfloat16).reshape(
            PAGES, LANES, HEAD_DIM
        )

    zero_row = jnp.zeros((LANES, HEAD_DIM), jnp.bfloat16)
    rows_vmem[pool_rows] = zero_row
    move_spots.wait()
    load_rows.wait()
    group = 16
    copies = [
        pltpu.make_async_copy(out_vmem.at[i], send_hbm.at[targets[i]], out_sem.at[i])
        for i in range(count)
    ]
    for i in range(count):

        def gather(c, carry):
            picked = [rows_vmem[spot_smem[i, c * group + u]] for u in range(group)]
            for u in range(group):
                out_vmem[i, c * group + u] = picked[u]
            return carry

        def clear(c, carry):
            for u in range(group):
                out_vmem[i, c * group + u] = zero_row
            return carry

        full = (count_smem[first + i] + group - 1) >> 4
        lax.fori_loop(0, full, gather, 0)
        lax.fori_loop(full, KEPT // group, clear, 0)
        copies[i].start()
    for copy in copies:
        copy.wait()


def pack(block_index, page_table, lengths, counts, order, positions, weights, cache_pool, blocks):
    count = page_table.shape[0]
    pool = cache_pool.shape[0]
    view = cache_pool.reshape(pool, PAGE, 2, HEADS_HERE, HEAD_DIM).transpose(0, 1, 3, 2, 4)
    as_rows = view.reshape(pool * PAGE, LANES, HEAD_DIM)
    as_flat = view.reshape(pool, PAGE * LANES, HEAD_DIM)
    requests = order.shape[0]
    hbm = lambda: pl.BlockSpec(memory_space=pltpu.HBM)
    operands = [
        page_table.T,
        lengths,
        counts,
        order.reshape(requests // 128, 128),
        positions,
        weights,
        as_rows,
        as_flat,
    ]
    operands = [pltpu.with_memory_space_constraint(x, pltpu.HBM) for x in operands]
    return pl.pallas_call(
        pack_kernel,
        out_shape=pltpu.HBM((blocks, SLOTS, LANES, HEAD_DIM), jnp.bfloat16),
        grid_spec=pltpu.PrefetchScalarGridSpec(
            num_scalar_prefetch=1,
            grid=(),
            in_specs=[hbm() for _ in operands],
            out_specs=hbm(),
            scratch_shapes=[
                pltpu.VMEM((pool * PAGE + 1, LANES, HEAD_DIM), jnp.bfloat16),
                pltpu.VMEM((pool, PAGE * LANES, HEAD_DIM), jnp.bfloat16),
                pltpu.VMEM((count, SLOTS, LANES, HEAD_DIM), jnp.bfloat16),
                pltpu.VMEM((count, CAP * LANES), jnp.float32),
                pltpu.VMEM((requests // 128, 128), jnp.int32),
                pltpu.VMEM((count, KEPT), jnp.int32),
                pltpu.VMEM((count, CAP), jnp.float32),
                pltpu.VMEM((count, KEPT), jnp.int32),
                pltpu.SMEM((PAGES, count), jnp.int32),
                pltpu.SMEM((requests,), jnp.int32),
                pltpu.SMEM((requests,), jnp.int32),
                pltpu.SMEM((count, KEPT), jnp.int32),
                pltpu.SemaphoreType.DMA((6,)),
                pltpu.SemaphoreType.DMA((2,)),
                pltpu.SemaphoreType.DMA(()),
                pltpu.SemaphoreType.DMA((count,)),
            ],
        ),
        compiler_params=pltpu.CompilerParams(vmem_limit_bytes=24 * 1024 * 1024),
        name="pack",
    )(jnp.reshape(block_index, (1,)), *operands)


def attend_kernel(
    source_ref,
    query_ref,
    key_ref,
    value_ref,
    bias_ref,
    weight_ref,
    recv_hbm,
    packed_hbm,
    share_ref,
    rows_vmem,
    score_vmem,
    attended_vmem,
    in_sem,
    out_sem,
):
    count = query_ref.shape[0]
    group = query_ref.shape[1]
    ins = [
        pltpu.make_async_copy(
            recv_hbm.at[source_ref[r]], rows_vmem.at[r, pl.ds(0, ROWS)], in_sem.at[r]
        )
        for r in range(count)
    ]
    outs = [
        pltpu.make_async_copy(rows_vmem.at[r, pl.ds(0, ROWS)], packed_hbm.at[r], out_sem.at[r])
        for r in range(count)
    ]
    for r in range(count):
        ins[r].start()
    for r in range(count):
        rows_vmem[r, pl.ds(ROWS, PAD_ROWS - ROWS)] = jnp.zeros(
            (PAD_ROWS - ROWS, HEAD_DIM), jnp.bfloat16
        )
    scale = HEAD_DIM ** (-0.5)
    contract_last = (((1,), (1,)), ((), ()))
    own_score = (
        jnp.sum(
            query_ref[...].astype(jnp.float32) * key_ref[...].astype(jnp.float32),
            axis=-1,
            keepdims=True,
        )
        * scale
    ).reshape(count * group, 1)
    for r in range(count):
        ins[r].wait()
        outs[r].start()
        scores = lax.dot_general(
            query_ref[r], rows_vmem[r], contract_last, preferred_element_type=jnp.float32
        )
        score_vmem[r * group : (r + 1) * group, :] = scores * scale + bias_ref[r]
    scores = score_vmem[...]
    highest = jnp.maximum(jnp.max(scores, axis=-1, keepdims=True), own_score)
    exponentials = jnp.exp(scores - highest)
    own_exp = jnp.exp(own_score - highest)
    denominator = jnp.sum(exponentials, axis=-1, keepdims=True) + own_exp
    probabilities = exponentials / denominator
    own_prob = (own_exp / denominator).astype(jnp.bfloat16).astype(jnp.float32)
    score_vmem[...] = pltpu.roll(probabilities, 1, axis=1)
    for r in range(count):
        moved = score_vmem[r * group : (r + 1) * group, :].astype(jnp.bfloat16)
        combined = jnp.dot(moved, rows_vmem[r], preferred_element_type=jnp.float32)
        attended_vmem[r] = combined + own_prob[
            r * group : (r + 1) * group
        ] * value_ref[r].astype(jnp.float32)
    attended = jnp.concatenate(
        [attended_vmem[:, h, :] for h in range(HEADS_HERE)], axis=1
    ).astype(jnp.bfloat16)
    share = jnp.dot(attended, weight_ref[...], preferred_element_type=jnp.float32).astype(
        jnp.bfloat16
    )
    width = share_ref.shape[2]
    for e in range(share_ref.shape[0]):
        share_ref[e] = share[:, e * width : (e + 1) * width]
    for r in range(count):
        outs[r].wait()


def attend(sources, queries, keys, values, bias, out_weight, recv, peers):
    count, group = queries.shape[:2]
    width = out_weight.shape[1] // peers
    whole = lambda: pl.BlockSpec(memory_space=pltpu.VMEM)
    hbm = lambda: pl.BlockSpec(memory_space=pltpu.HBM)
    return pl.pallas_call(
        attend_kernel,
        out_shape=(
            pltpu.HBM((count, ROWS, HEAD_DIM), jnp.bfloat16),
            jax.ShapeDtypeStruct((peers, count, width), jnp.bfloat16),
        ),
        grid_spec=pltpu.PrefetchScalarGridSpec(
            num_scalar_prefetch=1,
            grid=(),
            in_specs=[whole(), whole(), whole(), whole(), whole(), hbm()],
            out_specs=[hbm(), whole()],
            scratch_shapes=[
                pltpu.VMEM((count, PAD_ROWS, HEAD_DIM), jnp.bfloat16),
                pltpu.VMEM((count * group, PAD_ROWS), jnp.float32),
                pltpu.VMEM((count, group, HEAD_DIM), jnp.float32),
                pltpu.SemaphoreType.DMA((count,)),
                pltpu.SemaphoreType.DMA((count,)),
            ],
        ),
        compiler_params=pltpu.CompilerParams(vmem_limit_bytes=16 * 1024 * 1024),
        name="attend",
    )(sources, queries, keys, values, bias, out_weight, recv)


def local(
    hidden_in,
    qkv_weight,
    out_weight,
    cache_pool,
    page_table,
    request_order,
    request_lengths,
    retained_counts,
    retained_positions,
    blended_weight,
):
    rows_here = hidden_in.shape[0]
    head_width = qkv_weight.shape[2]
    heads_here = head_width // HEAD_DIM
    blocks = lax.axis_size("blk")
    peers = lax.axis_size("head")
    block_index = lax.axis_index("blk")
    first = block_index * rows_here
    slot_index = jnp.arange(KEPT, dtype=jnp.int32)
    take = lambda array: lax.dynamic_slice_in_dim(array, first, rows_here, 0)

    outgoing = pack(
        block_index,
        page_table,
        request_lengths,
        retained_counts,
        request_order,
        retained_positions,
        blended_weight,
        cache_pool,
        blocks,
    )
    outgoing = outgoing.reshape(blocks, ROWS, HEAD_DIM)
    arrived = lax.all_to_all(outgoing, "blk", split_axis=0, concat_axis=0, tiled=True)

    old_ids = take(request_order)
    sources = old_ids // rows_here
    lengths = request_lengths[old_ids]
    counts = retained_counts[old_ids]
    keep = jnp.where(slot_index[None, :] < counts[:, None], retained_positions[old_ids], CAP)
    spots = jnp.arange(CAP, dtype=jnp.int32)
    dropped = (spots[None, :] < lengths[:, None]) & jnp.logical_not(
        jnp.any(keep[:, :, None] == spots[None, None, :], axis=1)
    )
    dropped_weight = jnp.where(dropped, blended_weight[old_ids], 0.0)
    dropped_mass = jnp.log(1.0 + jnp.sum(dropped_weight.reshape(rows_here, PAGES, PAGE), axis=2))
    page_start = jnp.arange(PAGES, dtype=jnp.int32) * PAGE
    bias_slots = jnp.concatenate(
        [
            jnp.where(slot_index[None, :] < counts[:, None], 0.0, NEG),
            jnp.where(page_start[None, :] < lengths[:, None], dropped_mass, NEG),
        ],
        axis=1,
    )
    columns = jnp.arange(ROWS, dtype=jnp.int32) % LANES
    head_rows = jnp.arange(8, dtype=jnp.int32)
    bias = jnp.where(
        columns[None, None, :] == 2 * head_rows[None, :, None],
        jnp.repeat(bias_slots, LANES, axis=1)[:, None, :],
        NEG,
    )
    bias = jnp.pad(bias, ((0, 0), (0, 0), (0, PAD_ROWS - ROWS)), constant_values=NEG)

    gathered = lax.all_gather(hidden_in, "head", axis=1, tiled=True)
    normed = layer_norm(gathered.astype(jnp.float32)).astype(jnp.bfloat16)
    project = lambda index: jnp.dot(
        normed, qkv_weight[:, index], preferred_element_type=jnp.float32
    ).reshape(rows_here, heads_here, HEAD_DIM)
    pad_heads = lambda array: jnp.pad(
        array.astype(jnp.bfloat16), ((0, 0), (0, 8 - heads_here), (0, 0))
    )
    queries = pad_heads(rotate(project(0), lengths))
    new_keys = pad_heads(rotate(project(1), lengths))
    new_values = pad_heads(project(2))

    packed, share = attend(
        sources, queries, new_keys, new_values, bias, out_weight, arrived, peers
    )
    parts = lax.all_to_all(share, "head", split_axis=0, concat_axis=0, tiled=True)
    summed = jnp.sum(parts.astype(jnp.float32), axis=0)
    hidden_out = (hidden_in.astype(jnp.float32) + summed).astype(jnp.bfloat16)
    packed_cache = (
        packed.reshape(rows_here, SLOTS, heads_here, 2, HEAD_DIM)
        .transpose(0, 1, 3, 2, 4)
        .reshape(rows_here, SLOTS, 2, head_width)
    )
    return (hidden_out, packed_cache)


def solution(mesh):
    return jax.shard_map(
        local,
        mesh=mesh,
        in_specs=(
            P("blk", "head"),
            P(None, None, "head"),
            P("head", None),
            P("blk", None, None, "head"),
            P("blk", None),
            P(),
            P(),
            P(),
            P(),
            P(),
        ),
        out_specs=(P("blk", "head"), P("blk", None, None, "head")),
        check_vma=False,
    )
```

time: 169 us -> 139 us (0.82)
  Pallas kernels: 36.3 us -> 14.6 us
  local copies, waits for them, and re-layouts: 18.6 us -> 12.4 us
  waiting for transfers between devices: 64.7 us -> 62.8 us
    pallas_call x2, Pallas kernels: 36.3 us -> 14.6 us  [the longest x1 8.85 us: pack(): pl.pallas_call(pack_kernel, out_shape=pltpu.HBM((blocks, SLOTS, LANES, HE...]
    unnamed x16 -> x14, local copies, waits for them, and re-layouts: 4.91 us -> 0.03 us
    all_to_all x1, waiting for transfers between devices: 64.7 us -> 62.8 us  [local(): lax.all_to_all(outgoing, 'blk', split_axis=0, concat_axis=0, tiled=True)]
  transfers between devices with their start and end apart: 1 -> 1, of which waited for: 1 -> 1; matrix products, arithmetic and copies ran while one was open for 10% -> 14% of each run, Pallas kernels for 0% -> 0%
where the time goes in v2:
time: 139 us; the launch traced here: 138 us
  waiting for transfers between devices  62.8 us (45%)
  blocking collectives  28.2 us (20%)
  Pallas kernels  14.6 us (11%)
  local copies, waits for them, and re-layouts  12.4 us (9%)
  starting transfers between devices  12.1 us (9%)
  other arithmetic  4.1 us (3%)
  matrix products  2.82 us (2%)
    all_to_all x1, waiting for transfers between devices, local(): lax.all_to_all(outgoing, 'blk', split_axis=0, concat_axis=0, tiled=True)  62.8 us
    all_to_all x1, blocking collectives, local(): lax.all_to_all(share, 'head', split_axis=0, concat_axis=0, tiled=True)  14.4 us
    all_gather x1, blocking collectives, local(): gathered = lax.all_gather(hidden_in, 'head', axis=1, tiled=True)  13.9 us
    all_to_all x1, starting transfers between devices, local(): lax.all_to_all(outgoing, 'blk', split_axis=0, concat_axis=0, tiled=True)  12.1 us
    pallas_call x1, Pallas kernels, pack(): pl.pallas_call(pack_kernel, out_shape=pltpu.HBM((blocks, SLOTS, LANES, HE...  8.85 us
    dot_general x5, local copies, waits for them, and re-layouts, local(): jnp.dot(normed, qkv_weight[:, index], preferred_element_type=jnp.float32)  6.54 us
    pallas_call x1, Pallas kernels, attend(): pl.pallas_call(attend_kernel, out_shape=(pltpu.HBM((count, ROWS, HEAD_DIM...  5.77 us
    dot_general x3, matrix products, local(): jnp.dot(normed, qkv_weight[:, index], preferred_element_type=jnp.float32)  2.82 us
  transfers between devices with their start and end apart: 1, of which 1 were waited for; matrix products, arithmetic and copies ran while one was open for 14% of the time, Pallas kernels for 0%

profile of v2, /device:TPU:1, one launch (start us, length us, event | category | flops | bytes accessed | tf_op | source)
XLA Modules:
  0.0 138.0 jit_solution(4627454547676391100)
XLA Ops:
  0.6 8.9 %pack.1 = bf16[32,132,4,128]{3,2,1,0:T(4,128)(2,1)} custom-call(s32[1]{0:T(128)} %bitcast.11.block_ref, s32[4,16]{1,0:T(4,128)} %bitcast.48, s32[512]{0:T(512)} %length_hbm.1, s32[512]{0:T(512)} %count_hbm.1, s32[4,128]{1,0:T(4,128)} %bitcast.47, s32[512,128]{1,0:T(8,128)} %keep_hbm.1, f32[512,256]{1,0:T(8,128)} %weight_hbm.1, ...), custom_call_target="tpu_custom_call" | custom-call | tf_op jit(solution)/shard_map/pack/pallas_call | solution.py:210
  9.5 12.1 %all-to-all-start = ((bf16[32,528,128]{2,1,0:T(8,128)(2,1)}), bf16[32,528,128]{2,1,0:T(8,128)(2,1)}, u32[]{:S(2)}, u32[]{:S(2)}) async-start(bf16[32,528,128]{2,1,0:T(8,128)(2,1)} %bitcast.40), calls=%async_computation | async-start | bytes 8650752 | tf_op jit(solution)/shard_map/all_to_all | solution.py:383
  21.7 0.8 compare_select_fusion
  22.4 0.7 gather_fusion
  23.1 0.7 gather_fusion.1
  23.8 1.5 %gather_fusion.2 = s32[16,128]{1,0:T(8,128)S(1)} fusion(s32[512,128]{1,0:T(8,128)} %keep_hbm.1, s32[1024]{0:T(1024)S(1)} %pad_clamp_fusion), kind=kCustom, calls=%fused_computation.2 | custom fusion | bytes 16448 | tf_op jit(solution)/shard_map/gather | solution.py:389
  25.3 1.6 %gather_fusion.3 = f32[16,256]{1,0:T(8,128)S(1)} fusion(f32[512,256]{1,0:T(8,128)} %weight_hbm.1, s32[1024]{0:T(1024)S(1)} %pad_clamp_fusion), kind=kCustom, calls=%fused_computation.3 | custom fusion | bytes 32832 | tf_op jit(solution)/shard_map/gather | solution.py:394
  26.9 0.5 convert_element_type.35
  27.5 0.4 fusion
  28.8 3.1 %slice_bitcast_fusion = (bf16[256,2048]{0,1:T(8,128)(2,1)S(1)}, bf16[256,2048]{0,1:T(8,128)(2,1)S(1)}, bf16[256,2048]{0,1:T(8,128)(2,1)}) fusion(bf16[2048,3,256]{2,0,1:T(8,128)(2,1)} %param.11), kind=kLoop, calls=%fused_computation.6 | loop fusion | bytes 6291456 | tf_op jit(solution)/shard_map/dot_general | solution.py:415
  31.8 0.6 copy.40
  32.5 13.9 %all_gather.3 = bf16[16,2048]{1,0:T(8,128)(2,1)S(1)} all-gather(bf16[16,256]{1,0:T(8,128)(2,1)S(1)} %copy-done.4), channel_id=1, replica_groups=mesh['head'=8,'blk'=32] {'head'}, dimensions={1}, use_global_device_ids=true | all-gather | bytes 73728 | tf_op jit(solution)/shard_map/all_gather | solution.py:413
  46.7 0.4 fusion.17
  47.1 0.6 copy.59
  47.7 0.6 copy.34
  48.4 1.6 %copy.37 = bf16[256,2048]{1,0:T(8,128)(2,1)S(1)} copy(bf16[256,2048]{0,1:T(8,128)(2,1)} %get-tuple-element.8) | data formatting | bytes 2097152 | tf_op jit(solution)/shard_map/dot_general | solution.py:415
  50.1 0.7 pad.16.value_ref
  50.9 0.7 multiply_cosine_fusion
  51.6 1.2 fusion.21
  52.9 1.2 fusion.19
  54.4 62.8 %all-to-all-done.recv_hbm = bf16[32,528,128]{2,1,0:T(8,128)(2,1)} async-done(((bf16[32,528,128]{2,1,0:T(8,128)(2,1)}), bf16[32,528,128]{2,1,0:T(8,128)(2,1)}, u32[]{:S(2)}, u32[]{:S(2)}) %all-to-all-start) | async-done | bytes 4325408 | tf_op jit(solution)/shard_map/all_to_all | solution.py:383
  117.2 5.8 %attend.1 = (bf16[16,528,128]{2,1,0:T(8,128)(2,1)}, bf16[8,16,256]{2,1,0:T(8,128)(2,1)S(1)}) custom-call(s32[16]{0:T(128)S(1)} %get-tuple-element.20.source_ref, bf16[16,8,128]{2,1,0:T(8,128)(2,1)S(1)} %get-tuple-element.23.query_ref, bf16[16,8,128]{2,1,0:T(8,128)(2,1)S(1)} %get-tuple-element.24.key_ref, bf16[16,8,128]{2,1,0:T(8,128)(2,1)S(1)} %pad.16.value_ref, ...), custom_call_target="tpu_custom_call" | custom-call | tf_op jit(solution)/shard_map/attend/pallas_call | solution.py:325
  123.0 14.4 %all_to_all.10 = bf16[8,16,256]{2,1,0:T(8,128)(2,1)S(1)} all-to-all(bf16[8,16,256]{2,1,0:T(8,128)(2,1)S(1)} %get-tuple-element.4), channel_id=1, replica_groups=mesh['head'=8,'blk'=32] {'head'}, dimensions={0} | all-to-all | bytes 131072 | tf_op jit(solution)/shard_map/all_to_all | solution.py:428
  137.4 0.6 add_convert_fusion
  (43 shorter events, 1.7 us)
Async XLA Ops:
  9.5 12.9 %copy-start.1 = (s32[512]{0:T(512)S(1)}, s32[512]{0:T(512)}, u32[]{:S(2)}) copy-start(s32[512]{0:T(512)} %length_hbm.1) | copy-start | bytes 6148
  9.5 13.6 %copy-start.2 = (s32[512]{0:T(512)S(1)}, s32[512]{0:T(512)}, u32[]{:S(2)}) copy-start(s32[512]{0:T(512)} %count_hbm.1) | copy-start | bytes 6148
  9.5 107.7 %all-to-all-start = ((bf16[32,528,128]{2,1,0:T(8,128)(2,1)}), bf16[32,528,128]{2,1,0:T(8,128)(2,1)}, u32[]{:S(2)}, u32[]{:S(2)}) async-start(bf16[32,528,128]{2,1,0:T(8,128)(2,1)} %bitcast.40), calls=%async_computation | async-start | bytes 8650752 | tf_op jit(solution)/shard_map/all_to_all | solution.py:383
  28.8 3.7 %copy-start.4 = (bf16[16,256]{1,0:T(8,128)(2,1)S(1)}, bf16[16,256]{1,0:T(8,128)(2,1)}, u32[]{:S(2)}) copy-start(bf16[16,256]{1,0:T(8,128)(2,1)} %param.10) | copy-start | bytes 24580
  46.4 1.4 copy-start.3
  46.7 1.7 %copy-start.6 = (f32[16]{0:T(128)}, f32[16]{0:T(128)S(1)}, u32[]{:S(2)}) copy-start(f32[16]{0:T(128)S(1)} %add_rsqrt_fusion) | copy-start | bytes 196
  48.4 68.8 %copy-start = (bf16[256,2048]{1,0:T(8,128)(2,1)S(1)}, bf16[256,2048]{1,0:T(8,128)(2,1)}, u32[]{:S(2)}) copy-start(bf16[256,2048]{1,0:T(8,128)(2,1)} %weight_ref.1) | copy-start | bytes 3145732
  54.2 83.2 %copy-start.5 = (bf16[16,256]{1,0:T(8,128)(2,1)S(1)}, bf16[16,256]{1,0:T(8,128)(2,1)}, u32[]{:S(2)}) copy-start(bf16[16,256]{1,0:T(8,128)(2,1)} %param.10) | copy-start | bytes 24580

commit v3 on v2

--- a/solution.py
+++ b/solution.py
@@ -73,6 +73,7 @@
     out_sem,
 ):
     count = keep_vmem.shape[0]
+    group = 16
     pool_rows = cache_rows_hbm.shape[0]
     first = pl.multiple_of(block_ref[0] * count, count)
     small = [
@@ -95,9 +96,9 @@
     )
     load_flat = pltpu.make_async_copy(cache_flat_hbm, flat_vmem, load_sem.at[1])
     load_rows.start()
-    load_flat.start()
     for copy in small:
         copy.wait()
+    load_flat.start()
 
     keep = keep_vmem[...]
     slot_id = lax.broadcasted_iota(jnp.int32, keep.shape, 1)
@@ -144,6 +145,32 @@
     same = (out_row & (LANES - 1)) == (out_lane & (LANES - 1))
     selectors = [jnp.where(same & (out_row >> 2 == j), 1.0, 0.0) for j in range(PAGES)]
 
+    zero_rows = jnp.zeros((group, LANES, HEAD_DIM), jnp.bfloat16)
+    rows_vmem[pool_rows] = zero_rows[0]
+
+    def clear(c, carry):
+        for i in range(count):
+            out_vmem[i, pl.ds(pl.multiple_of(c * group, group), group)] = zero_rows
+        return carry
+
+    lax.fori_loop(0, KEPT // group, clear, 0)
+    move_spots.wait()
+    load_rows.wait()
+    for i in range(count):
+
+        def gather(c, carry):
+            picked = [rows_vmem[spot_smem[i, c * group + u]] for u in range(group)]
+            for u in range(group):
+                out_vmem[i, c * group + u] = picked[u]
+            return carry
+
+        full = (count_smem[first + i] + group - 1) >> 4
+        lax.fori_loop(0, full, gather, 0)
+
+    copies = [
+        pltpu.make_async_copy(out_vmem.at[i], send_hbm.at[targets[i]], out_sem.at[i])
+        for i in range(count)
+    ]
     load_flat.wait()
     for i in range(count):
         merged = jnp.zeros((PAGES * LANES, HEAD_DIM), jnp.float32)
@@ -157,32 +184,6 @@
         out_vmem[i, pl.ds(KEPT, PAGES)] = merged.astype(jnp.bfloat16).reshape(
             PAGES, LANES, HEAD_DIM
         )
-
-    zero_row = jnp.zeros((LANES, HEAD_DIM), jnp.bfloat16)
-    rows_vmem[pool_rows] = zero_row
-    move_spots.wait()
-    load_rows.wait()
-    group = 16
-    copies = [
-        pltpu.make_async_copy(out_vmem.at[i], send_hbm.at[targets[i]], out_sem.at[i])
-        for i in range(count)
-    ]
-    for i in range(count):
-
-        def gather(c, carry):
-            picked = [rows_vmem[spot_smem[i, c * group + u]] for u in range(group)]
-            for u in range(group):
-                out_vmem[i, c * group + u] = picked[u]
-            return carry
-
-        def clear(c, carry):
-            for u in range(group):
-                out_vmem[i, c * group + u] = zero_row
-            return carry
-
-        full = (count_smem[first + i] + group - 1) >> 4
-        lax.fori_loop(0, full, gather, 0)
-        lax.fori_loop(full, KEPT // group, clear, 0)
         copies[i].start()
     for copy in copies:
         copy.wait()

time: 139 us -> 137 us (0.986)
  no operation moved by 1% of the time
where the time goes in v3:
time: 137 us
  waiting for transfers between devices  62.8 us (46%)
  blocking collectives  28.2 us (21%)
  Pallas kernels  13.4 us (10%)
  local copies, waits for them, and re-layouts  12.4 us (9%)
  starting transfers between devices  12.2 us (9%)
  other arithmetic  4.1 us (3%)
  matrix products  2.82 us (2%)
    all_to_all x1, waiting for transfers between devices, local(): lax.all_to_all(outgoing, 'blk', split_axis=0, concat_axis=0, tiled=True)  62.8 us
    all_to_all x1, blocking collectives, local(): lax.all_to_all(share, 'head', split_axis=0, concat_axis=0, tiled=True)  14.4 us
    all_gather x1, blocking collectives, local(): gathered = lax.all_gather(hidden_in, 'head', axis=1, tiled=True)  13.9 us
    all_to_all x1, starting transfers between devices, local(): lax.all_to_all(outgoing, 'blk', split_axis=0, concat_axis=0, tiled=True)  12.2 us
    pallas_call x1, Pallas kernels, pack(): pl.pallas_call(pack_kernel, out_shape=pltpu.HBM((blocks, SLOTS, LANES, HE...  7.65 us
    dot_general x5, local copies, waits for them, and re-layouts, local(): jnp.dot(normed, qkv_weight[:, index], preferred_element_type=jnp.float32)  6.54 us
    pallas_call x1, Pallas kernels, attend(): pl.pallas_call(attend_kernel, out_shape=(pltpu.HBM((count, ROWS, HEAD_DIM...  5.77 us
    dot_general x3, matrix products, local(): jnp.dot(normed, qkv_weight[:, index], preferred_element_type=jnp.float32)  2.82 us
  transfers between devices with their start and end apart: 1, of which 1 were waited for; matrix products, arithmetic and copies ran while one was open for 14% of the time, Pallas kernels for 0%

profile of v3, /device:TPU:1, one launch (start us, length us, event | category | flops | bytes accessed | tf_op | source)
XLA Modules:
  0.0 136.9 jit_solution(9247554710610617370)
XLA Ops:
  0.6 7.6 %pack.1 = bf16[32,132,4,128]{3,2,1,0:T(4,128)(2,1)} custom-call(s32[1]{0:T(128)} %bitcast.11.block_ref, s32[4,16]{1,0:T(4,128)} %bitcast.48, s32[512]{0:T(512)} %length_hbm.1, s32[512]{0:T(512)} %count_hbm.1, s32[4,128]{1,0:T(4,128)} %bitcast.47, s32[512,128]{1,0:T(8,128)} %keep_hbm.1, f32[512,256]{1,0:T(8,128)} %weight_hbm.1, ...), custom_call_target="tpu_custom_call" | custom-call | tf_op jit(solution)/shard_map/pack/pallas_call | solution.py:211
  8.3 12.2 %all-to-all-start = ((bf16[32,528,128]{2,1,0:T(8,128)(2,1)}), bf16[32,528,128]{2,1,0:T(8,128)(2,1)}, u32[]{:S(2)}, u32[]{:S(2)}) async-start(bf16[32,528,128]{2,1,0:T(8,128)(2,1)} %bitcast.40), calls=%async_computation | async-start | bytes 8650752 | tf_op jit(solution)/shard_map/all_to_all | solution.py:384
  20.6 0.8 compare_select_fusion
  21.4 0.7 gather_fusion
  22.0 0.7 gather_fusion.1
  22.7 1.5 %gather_fusion.2 = s32[16,128]{1,0:T(8,128)S(1)} fusion(s32[512,128]{1,0:T(8,128)} %keep_hbm.1, s32[1024]{0:T(1024)S(1)} %pad_clamp_fusion), kind=kCustom, calls=%fused_computation.2 | custom fusion | bytes 16448 | tf_op jit(solution)/shard_map/gather | solution.py:390
  24.2 1.6 %gather_fusion.3 = f32[16,256]{1,0:T(8,128)S(1)} fusion(f32[512,256]{1,0:T(8,128)} %weight_hbm.1, s32[1024]{0:T(1024)S(1)} %pad_clamp_fusion), kind=kCustom, calls=%fused_computation.3 | custom fusion | bytes 32832 | tf_op jit(solution)/shard_map/gather | solution.py:395
  25.8 0.5 convert_element_type.35
  26.4 0.4 fusion
  27.7 3.1 %slice_bitcast_fusion = (bf16[256,2048]{0,1:T(8,128)(2,1)S(1)}, bf16[256,2048]{0,1:T(8,128)(2,1)S(1)}, bf16[256,2048]{0,1:T(8,128)(2,1)}) fusion(bf16[2048,3,256]{2,0,1:T(8,128)(2,1)} %param.11), kind=kLoop, calls=%fused_computation.6 | loop fusion | bytes 6291456 | tf_op jit(solution)/shard_map/dot_general | solution.py:416
  30.7 0.6 copy.40
  31.4 13.9 %all_gather.3 = bf16[16,2048]{1,0:T(8,128)(2,1)S(1)} all-gather(bf16[16,256]{1,0:T(8,128)(2,1)S(1)} %copy-done.4), channel_id=1, replica_groups=mesh['head'=8,'blk'=32] {'head'}, dimensions={1}, use_global_device_ids=true | all-gather | bytes 73728 | tf_op jit(solution)/shard_map/all_gather | solution.py:414
  45.6 0.4 fusion.17
  46.0 0.6 copy.59
  46.6 0.6 copy.34
  47.3 1.6 %copy.37 = bf16[256,2048]{1,0:T(8,128)(2,1)S(1)} copy(bf16[256,2048]{0,1:T(8,128)(2,1)} %get-tuple-element.8) | data formatting | bytes 2097152 | tf_op jit(solution)/shard_map/dot_general | solution.py:416
  49.1 0.7 pad.16.value_ref
  49.8 0.7 multiply_cosine_fusion
  50.5 1.2 fusion.21
  51.8 1.2 fusion.19
  53.3 62.8 %all-to-all-done.recv_hbm = bf16[32,528,128]{2,1,0:T(8,128)(2,1)} async-done(((bf16[32,528,128]{2,1,0:T(8,128)(2,1)}), bf16[32,528,128]{2,1,0:T(8,128)(2,1)}, u32[]{:S(2)}, u32[]{:S(2)}) %all-to-all-start) | async-done | bytes 4325408 | tf_op jit(solution)/shard_map/all_to_all | solution.py:384
  116.1 5.8 %attend.1 = (bf16[16,528,128]{2,1,0:T(8,128)(2,1)}, bf16[8,16,256]{2,1,0:T(8,128)(2,1)S(1)}) custom-call(s32[16]{0:T(128)S(1)} %get-tuple-element.20.source_ref, bf16[16,8,128]{2,1,0:T(8,128)(2,1)S(1)} %get-tuple-element.23.query_ref, bf16[16,8,128]{2,1,0:T(8,128)(2,1)S(1)} %get-tuple-element.24.key_ref, bf16[16,8,128]{2,1,0:T(8,128)(2,1)S(1)} %pad.16.value_ref, ...), custom_call_target="tpu_custom_call" | custom-call | tf_op jit(solution)/shard_map/attend/pallas_call | solution.py:326
  121.9 14.4 %all_to_all.10 = bf16[8,16,256]{2,1,0:T(8,128)(2,1)S(1)} all-to-all(bf16[8,16,256]{2,1,0:T(8,128)(2,1)S(1)} %get-tuple-element.4), channel_id=1, replica_groups=mesh['head'=8,'blk'=32] {'head'}, dimensions={0} | all-to-all | bytes 131072 | tf_op jit(solution)/shard_map/all_to_all | solution.py:429
  136.3 0.6 add_convert_fusion
  (43 shorter events, 1.7 us)
Async XLA Ops:
  8.3 13.1 %copy-start.1 = (s32[512]{0:T(512)S(1)}, s32[512]{0:T(512)}, u32[]{:S(2)}) copy-start(s32[512]{0:T(512)} %length_hbm.1) | copy-start | bytes 6148
  8.3 13.7 %copy-start.2 = (s32[512]{0:T(512)S(1)}, s32[512]{0:T(512)}, u32[]{:S(2)}) copy-start(s32[512]{0:T(512)} %count_hbm.1) | copy-start | bytes 6148
  8.3 107.8 %all-to-all-start = ((bf16[32,528,128]{2,1,0:T(8,128)(2,1)}), bf16[32,528,128]{2,1,0:T(8,128)(2,1)}, u32[]{:S(2)}, u32[]{:S(2)}) async-start(bf16[32,528,128]{2,1,0:T(8,128)(2,1)} %bitcast.40), calls=%async_computation | async-start | bytes 8650752 | tf_op jit(solution)/shard_map/all_to_all | solution.py:384
  27.7 3.7 %copy-start.4 = (bf16[16,256]{1,0:T(8,128)(2,1)S(1)}, bf16[16,256]{1,0:T(8,128)(2,1)}, u32[]{:S(2)}) copy-start(bf16[16,256]{1,0:T(8,128)(2,1)} %param.10) | copy-start | bytes 24580
  45.3 1.4 copy-start.3
  45.6 1.7 %copy-start.6 = (f32[16]{0:T(128)}, f32[16]{0:T(128)S(1)}, u32[]{:S(2)}) copy-start(f32[16]{0:T(128)S(1)} %add_rsqrt_fusion) | copy-start | bytes 196
  47.3 68.8 %copy-start = (bf16[256,2048]{1,0:T(8,128)(2,1)S(1)}, bf16[256,2048]{1,0:T(8,128)(2,1)}, u32[]{:S(2)}) copy-start(bf16[256,2048]{1,0:T(8,128)(2,1)} %weight_ref.1) | copy-start | bytes 3145732
  53.1 83.2 %copy-start.5 = (bf16[16,256]{1,0:T(8,128)(2,1)S(1)}, bf16[16,256]{1,0:T(8,128)(2,1)}, u32[]{:S(2)}) copy-start(bf16[16,256]{1,0:T(8,128)(2,1)} %param.10) | copy-start | bytes 24580

commit v4 on v3

--- a/solution.py
+++ b/solution.py
@@ -16,6 +16,9 @@
 ROWS = SLOTS * LANES
 PAD_ROWS = 640
 NEG = -1e30
+ROUND_ONE = 54
+ROUND_TWO = 36
+STEP = 6
 
 epsilon = 1e-05
 
@@ -347,6 +350,479 @@
     )(sources, queries, keys, values, bias, out_weight, recv)
 
 
+def spread_kernel(
+    block_ref,
+    page_hbm,
+    length_hbm,
+    count_hbm,
+    order_hbm,
+    keep_hbm,
+    weight_hbm,
+    cache_rows_hbm,
+    send_hbm,
+    rows_vmem,
+    out_vmem,
+    wide_vmem,
+    order_vmem,
+    keep_vmem,
+    weight_vmem,
+    spot_vmem,
+    dest_vmem,
+    page_smem,
+    length_smem,
+    count_smem,
+    spot_smem,
+    dest_smem,
+    used_smem,
+    free_smem,
+    small_sem,
+    load_sem,
+    spot_sem,
+    dest_sem,
+    out_sem,
+):
+    count = keep_vmem.shape[0]
+    group = 16
+    pool_rows = cache_rows_hbm.shape[0]
+    slots = send_hbm.shape[0] // ROUND_ONE
+    relays = slots - count
+    shift = relays.bit_length() - 1
+    first = pl.multiple_of(block_ref[0] * count, count)
+    small = [
+        pltpu.make_async_copy(source, target, small_sem.at[n])
+        for n, (source, target) in enumerate(
+            [
+                (keep_hbm.at[pl.ds(first, count)], keep_vmem),
+                (count_hbm, count_smem),
+                (page_hbm, page_smem),
+                (order_hbm, order_vmem),
+                (length_hbm, length_smem),
+                (weight_hbm.at[pl.ds(first, count)], weight_vmem),
+            ]
+        )
+    ]
+    for copy in small:
+        copy.start()
+    load_rows = pltpu.make_async_copy(
+        cache_rows_hbm, rows_vmem.at[pl.ds(0, pool_rows)], load_sem
+    )
+    load_rows.start()
+    for copy in small:
+        copy.wait()
+
+    order = order_vmem[...]
+    place = (
+        lax.broadcasted_iota(jnp.int32, order.shape, 0) * order.shape[1]
+        + lax.broadcasted_iota(jnp.int32, order.shape, 1)
+    ) // count
+    targets = [jnp.sum(jnp.where(order == first + i, place, 0)) for i in range(count)]
+
+    keep = keep_vmem[...]
+    slot_id = lax.broadcasted_iota(jnp.int32, keep.shape, 1)
+    row_id = lax.broadcasted_iota(jnp.int32, keep.shape, 0)
+    counts = jnp.zeros(keep.shape, jnp.int32)
+    base = jnp.zeros(keep.shape, jnp.int32)
+    target = jnp.zeros(keep.shape, jnp.int32)
+    page_of = keep >> 6
+    for i in range(count):
+        here = row_id == i
+        counts = jnp.where(here, count_smem[first + i], counts)
+        target = jnp.where(here, targets[i], target)
+        for j in range(PAGES):
+            base = jnp.where(here & (page_of == j), page_smem[j, i] * PAGE, base)
+    keep = jnp.where(slot_id < counts, keep, CAP)
+    spot_vmem[...] = jnp.where(slot_id < counts, base + (keep & (PAGE - 1)), pool_rows)
+    move_spots = pltpu.make_async_copy(spot_vmem, spot_smem, spot_sem)
+    move_spots.start()
+
+    for m in range(slots):
+        used_smem[m] = 0
+    for i in range(count):
+        used_smem[targets[i]] = 1
+    free = 0
+    for m in range(slots):
+        free_smem[free] = m
+        free = free + 1 - used_smem[m]
+    before = jnp.zeros(keep.shape, jnp.int32)
+    for i in range(count):
+        beyond = jnp.maximum(count_smem[first + i] + PAGES - ROUND_ONE, 0)
+        before = before + jnp.where(target > targets[i], beyond, 0)
+    entry = slot_id + PAGES
+    ordinal = jnp.maximum(before + entry - ROUND_ONE, 0)
+    turn = ordinal & (relays - 1)
+    relay = jnp.zeros(keep.shape, jnp.int32)
+    for j in range(relays):
+        relay = jnp.where(turn == j, free_smem[j], relay)
+    depth = jnp.minimum(ordinal >> shift, ROUND_ONE - 1)
+    dest = jnp.where(
+        entry < ROUND_ONE, target * ROUND_ONE + entry, relay * ROUND_ONE + depth
+    )
+    dest_vmem[...] = jnp.where(slot_id < counts, dest, slots * ROUND_ONE)
+    move_dests = pltpu.make_async_copy(dest_vmem, dest_smem, dest_sem)
+    move_dests.start()
+
+    keep_cols = jnp.transpose(keep.astype(jnp.float32))
+    lane_pos = lax.broadcasted_iota(jnp.int32, (KEPT, CAP), 1).astype(jnp.float32)
+    spot = lax.broadcasted_iota(jnp.int32, (1, CAP), 1)
+    factors = []
+    for i in range(count):
+        match = keep_cols[:, i : i + 1] == lane_pos
+        kept = jnp.max(jnp.where(match, 1.0, 0.0), axis=0, keepdims=True)
+        dropped = (spot < length_smem[first + i]) & (kept < 0.5)
+        factors.append(jnp.where(dropped, weight_vmem[i : i + 1, :], 0.0))
+    factors = jnp.concatenate(factors, axis=0).astype(jnp.bfloat16)
+    repeat = (
+        lax.broadcasted_iota(jnp.int32, (CAP, CAP * LANES), 1) >> 2
+        == lax.broadcasted_iota(jnp.int32, (CAP, CAP * LANES), 0)
+    )
+    repeat = jnp.where(repeat, 1.0, 0.0).astype(jnp.bfloat16)
+    wide_vmem[...] = jnp.dot(factors, repeat, preferred_element_type=jnp.float32)
+    page_lanes = PAGE * LANES
+    out_row = lax.broadcasted_iota(jnp.int32, (PAGES * LANES, page_lanes), 0)
+    out_lane = lax.broadcasted_iota(jnp.int32, (PAGES * LANES, page_lanes), 1)
+    same = (out_row & (LANES - 1)) == (out_lane & (LANES - 1))
+    selectors = [jnp.where(same & (out_row >> 2 == j), 1.0, 0.0) for j in range(PAGES)]
+
+    zero_rows = jnp.zeros((group, LANES, HEAD_DIM), jnp.bfloat16)
+    rows_vmem[pl.ds(pool_rows, 8)] = zero_rows[:8]
+
+    def clear(c, carry):
+        for u in range(4):
+            out_vmem[pl.ds(pl.multiple_of((c * 4 + u) * group, group), group)] = zero_rows
+        return carry
+
+    lax.fori_loop(0, slots * ROUND_ONE // (4 * group), clear, 0)
+    move_spots.wait()
+    move_dests.wait()
+    load_rows.wait()
+    for i in range(count):
+
+        def gather(c, carry):
+            picked = [rows_vmem[spot_smem[i, c * group + u]] for u in range(group)]
+            for u in range(group):
+                out_vmem[dest_smem[i, c * group + u]] = picked[u]
+            return carry
+
+        lax.fori_loop(0, (count_smem[first + i] + group - 1) >> 4, gather, 0)
+
+    flat = rows_vmem.reshape(rows_vmem.shape[0] * LANES, HEAD_DIM)
+    for i in range(count):
+        merged = jnp.zeros((PAGES * LANES, HEAD_DIM), jnp.float32)
+        for j in range(PAGES):
+            wide = wide_vmem[i : i + 1, j * page_lanes : (j + 1) * page_lanes]
+            start = pl.multiple_of(page_smem[j, i] * page_lanes, page_lanes)
+            merged = merged + jnp.dot(
+                (selectors[j] * wide).astype(jnp.bfloat16),
+                flat[pl.ds(start, page_lanes)],
+                preferred_element_type=jnp.float32,
+            )
+        out_vmem[pl.ds(targets[i] * ROUND_ONE, PAGES)] = merged.astype(jnp.bfloat16).reshape(
+            PAGES, LANES, HEAD_DIM
+        )
+    out = pltpu.make_async_copy(out_vmem.at[pl.ds(0, slots * ROUND_ONE)], send_hbm, out_sem)
+    out.start()
+    out.wait()
+
+
+def spread(block_index, page_table, lengths, counts, order, positions, weights, cache_pool, blocks):
+    count = page_table.shape[0]
+    pool = cache_pool.shape[0]
+    view = cache_pool.reshape(pool, PAGE, 2, HEADS_HERE, HEAD_DIM).transpose(0, 1, 3, 2, 4)
+    as_rows = view.reshape(pool * PAGE, LANES, HEAD_DIM)
+    requests = order.shape[0]
+    hbm = lambda: pl.BlockSpec(memory_space=pltpu.HBM)
+    operands = [
+        page_table.T,
+        lengths,
+        counts,
+        order.reshape(requests // 128, 128),
+        positions,
+        weights,
+        as_rows,
+    ]
+    operands = [pltpu.with_memory_space_constraint(x, pltpu.HBM) for x in operands]
+    return pl.pallas_call(
+        spread_kernel,
+        out_shape=pltpu.HBM((blocks * ROUND_ONE, LANES, HEAD_DIM), jnp.bfloat16),
+        grid_spec=pltpu.PrefetchScalarGridSpec(
+            num_scalar_prefetch=1,
+            grid=(),
+            in_specs=[hbm() for _ in operands],
+            out_specs=hbm(),
+            scratch_shapes=[
+                pltpu.VMEM((pool * PAGE + 8, LANES, HEAD_DIM), jnp.bfloat16),
+                pltpu.VMEM((blocks * ROUND_ONE + 8, LANES, HEAD_DIM), jnp.bfloat16),
+                pltpu.VMEM((count, CAP * LANES), jnp.float32),
+                pltpu.VMEM((requests // 128, 128), jnp.int32),
+                pltpu.VMEM((count, KEPT), jnp.int32),
+                pltpu.VMEM((count, CAP), jnp.float32),
+                pltpu.VMEM((count, KEPT), jnp.int32),
+                pltpu.VMEM((count, KEPT), jnp.int32),
+                pltpu.SMEM((PAGES, count), jnp.int32),
+                pltpu.SMEM((requests,), jnp.int32),
+                pltpu.SMEM((requests,), jnp.int32),
+                pltpu.SMEM((count, KEPT), jnp.int32),
+                pltpu.SMEM((count, KEPT), jnp.int32),
+                pltpu.SMEM((blocks,), jnp.int32),
+                pltpu.SMEM((blocks + 1,), jnp.int32),
+                pltpu.SemaphoreType.DMA((6,)),
+                pltpu.SemaphoreType.DMA(()),
+                pltpu.SemaphoreType.DMA(()),
+                pltpu.SemaphoreType.DMA(()),
+                pltpu.SemaphoreType.DMA(()),
+            ],
+        ),
+        compiler_params=pltpu.CompilerParams(vmem_limit_bytes=20 * 1024 * 1024),
+        name="spread",
+    )(jnp.reshape(block_index, (1,)), *operands)
+
+
+def relay_kernel(held_ref, dest_ref, recv_ref, send_hbm, out_vmem, out_sem):
+    slots = held_ref.shape[0]
+
+    def source(s, carry):
+        def forward(c, inner):
+            start = s * ROUND_ONE + c * STEP
+            picked = [recv_ref[start + u] for u in range(STEP)]
+            for u in range(STEP):
+                out_vmem[dest_ref[s, c * STEP + u]] = picked[u]
+            return inner
+
+        lax.fori_loop(0, lax.div(held_ref[s] + (STEP - 1), STEP), forward, 0)
+        return carry
+
+    lax.fori_loop(0, slots, source, 0)
+    out = pltpu.make_async_copy(out_vmem.at[pl.ds(0, slots * ROUND_TWO)], send_hbm, out_sem)
+    out.start()
+    out.wait()
+
+
+def forward_rows(held, dest, recv, blocks):
+    return pl.pallas_call(
+        relay_kernel,
+        out_shape=pltpu.HBM((blocks * ROUND_TWO, LANES, HEAD_DIM), jnp.bfloat16),
+        grid_spec=pltpu.PrefetchScalarGridSpec(
+            num_scalar_prefetch=2,
+            grid=(),
+            in_specs=[pl.BlockSpec(memory_space=pltpu.VMEM)],
+            out_specs=pl.BlockSpec(memory_space=pltpu.HBM),
+            scratch_shapes=[
+                pltpu.VMEM((blocks * ROUND_TWO + 8, LANES, HEAD_DIM), jnp.bfloat16),
+                pltpu.SemaphoreType.DMA(()),
+            ],
+        ),
+        compiler_params=pltpu.CompilerParams(vmem_limit_bytes=12 * 1024 * 1024),
+        name="relay",
+    )(held, dest, recv)
+
+
+def gather_attend_kernel(
+    source_ref,
+    beyond_ref,
+    place_ref,
+    query_ref,
+    key_ref,
+    value_ref,
+    bias_ref,
+    weight_ref,
+    direct_ref,
+    relayed_ref,
+    packed_hbm,
+    share_ref,
+    rows_vmem,
+    score_vmem,
+    attended_vmem,
+    out_sem,
+):
+    count, group = query_ref.shape[:2]
+    head = ROUND_ONE - PAGES
+    zero_rows = jnp.zeros((8, LANES, HEAD_DIM), jnp.bfloat16)
+    for r in range(count):
+        for c in range(head, KEPT, 8):
+            rows_vmem[pl.ds(r * SLOTS + min(c, KEPT - 8), 8)] = zero_rows
+    for c in range((rows_vmem.shape[0] - count * SLOTS) // 8):
+        rows_vmem[pl.ds(count * SLOTS + c * 8, 8)] = zero_rows
+    scale = HEAD_DIM ** (-0.5)
+    contract_last = (((1,), (1,)), ((), ()))
+    own_score = (
+        jnp.sum(
+            query_ref[...].astype(jnp.float32) * key_ref[...].astype(jnp.float32),
+            axis=-1,
+            keepdims=True,
+        )
+        * scale
+    ).reshape(count * group, 1)
+    outs = [
+        pltpu.make_async_copy(
+            rows_vmem.at[pl.ds(r * SLOTS, SLOTS)],
+            packed_hbm.at[pl.ds(r * SLOTS, SLOTS)],
+            out_sem.at[r],
+        )
+        for r in range(count)
+    ]
+    for r in range(count):
+        source = source_ref[r]
+        beyond = beyond_ref[source]
+        start = source * ROUND_ONE
+        rows_vmem[pl.ds(r * SLOTS, head)] = direct_ref[pl.ds(start + PAGES, head)]
+        rows_vmem[pl.ds(r * SLOTS + KEPT, PAGES)] = direct_ref[pl.ds(start, PAGES)]
+
+        def place(c, carry):
+            picked = [relayed_ref[place_ref[source, c * STEP + u]] for u in range(STEP)]
+            for u in range(STEP):
+                past = c * STEP + u >= beyond
+                rows_vmem[r * SLOTS + head + c * STEP + u] = jnp.where(
+                    past, zero_rows[0], picked[u]
+                )
+            return carry
+
+        lax.fori_loop(0, lax.div(beyond + (STEP - 1), STEP), place, 0)
+        outs[r].start()
+    flat = rows_vmem.reshape(rows_vmem.shape[0] * LANES, HEAD_DIM)
+    for r in range(count):
+        scores = lax.dot_general(
+            query_ref[r],
+            flat[pl.ds(r * ROWS, PAD_ROWS)],
+            contract_last,
+            preferred_element_type=jnp.float32,
+        )
+        score_vmem[r * group : (r + 1) * group, :] = scores * scale + bias_ref[r]
+    scores = score_vmem[...]
+    highest = jnp.maximum(jnp.max(scores, axis=-1, keepdims=True), own_score)
+    exponentials = jnp.exp(scores - highest)
+    own_exp = jnp.exp(own_score - highest)
+    denominator = jnp.sum(exponentials, axis=-1, keepdims=True) + own_exp
+    probabilities = exponentials / denominator
+    own_prob = (own_exp / denominator).astype(jnp.bfloat16).astype(jnp.float32)
+    score_vmem[...] = pltpu.roll(probabilities, 1, axis=1)
+    for r in range(count):
+        moved = score_vmem[r * group : (r + 1) * group, :].astype(jnp.bfloat16)
+        combined = jnp.dot(
+            moved, flat[pl.ds(r * ROWS, PAD_ROWS)], preferred_element_type=jnp.float32
+        )
+        attended_vmem[r] = combined + own_prob[
+            r * group : (r + 1) * group
+        ] * value_ref[r].astype(jnp.float32)
+    attended = jnp.concatenate(
+        [attended_vmem[:, h, :] for h in range(HEADS_HERE)], axis=1
+    ).astype(jnp.bfloat16)
+    share = jnp.dot(attended, weight_ref[...], preferred_element_type=jnp.float32).astype(
+        jnp.bfloat16
+    )
+    width = share_ref.shape[2]
+    for e in range(share_ref.shape[0]):
+        share_ref[e] = share[:, e * width : (e + 1) * width]
+    for r in range(count):
+        outs[r].wait()
+
+
+def gather_attend(
+    sources, beyond, places, queries, keys, values, bias, out_weight, direct, relayed, peers
+):
+    count, group = queries.shape[:2]
+    width = out_weight.shape[1] // peers
+    whole = lambda: pl.BlockSpec(memory_space=pltpu.VMEM)
+    hbm = lambda: pl.BlockSpec(memory_space=pltpu.HBM)
+    spare = -(-(PAD_ROWS - ROWS) // (8 * LANES)) * 8
+    return pl.pallas_call(
+        gather_attend_kernel,
+        out_shape=(
+            pltpu.HBM((count * SLOTS, LANES, HEAD_DIM), jnp.bfloat16),
+            jax.ShapeDtypeStruct((peers, count, width), jnp.bfloat16),
+        ),
+        grid_spec=pltpu.PrefetchScalarGridSpec(
+            num_scalar_prefetch=3,
+            grid=(),
+            in_specs=[whole() for _ in range(7)],
+            out_specs=[hbm(), whole()],
+            scratch_shapes=[
+                pltpu.VMEM((count * SLOTS + spare, LANES, HEAD_DIM), jnp.bfloat16),
+                pltpu.VMEM((count * group, PAD_ROWS), jnp.float32),
+                pltpu.VMEM((count, group, HEAD_DIM), jnp.float32),
+                pltpu.SemaphoreType.DMA((count,)),
+            ],
+        ),
+        compiler_params=pltpu.CompilerParams(vmem_limit_bytes=16 * 1024 * 1024),
+        name="gather_attend",
+    )(
+        sources,
+        beyond,
+        places,
+        queries,
+        keys,
+        values,
+        bias,
+        out_weight,
+        direct,
+        relayed,
+    )
+
+
+def routes(request_order, retained_counts, block_index, blocks, rows_here):
+    relays = blocks - rows_here
+    shift = relays.bit_length() - 1
+    ids = jnp.arange(request_order.shape[0], dtype=jnp.int32)
+    line = jnp.arange(blocks, dtype=jnp.int32)
+    target_of = jnp.sum(
+        jnp.where(request_order[None, :] == ids[:, None], (ids // rows_here)[None, :], 0), axis=1
+    ).reshape(blocks, rows_here)
+    rows = retained_counts.reshape(blocks, rows_here) + PAGES
+    sent = jnp.sum(
+        jnp.where(target_of[:, :, None] == line[None, None, :], rows[:, :, None], 0), axis=1
+    )
+    free = sent == 0
+    beyond = jnp.maximum(sent - ROUND_ONE, 0)
+    lower = line[None, :] < line[:, None]
+    prefix = lambda array: jnp.sum(jnp.where(lower[None], array[:, None, :], 0), axis=2)
+    start = prefix(beyond)
+    rank = prefix(free.astype(jnp.int32))
+    total = jnp.sum(beyond, axis=1)
+    until = lambda ordinal, turn: (ordinal - turn + (relays - 1)) >> shift
+    above = lambda array: jnp.sum(jnp.where(lower[:, :, None], array[None], 0), axis=1)
+    pick = lambda array: jnp.sum(jnp.where(line[None, :] == block_index, array, 0), axis=1)
+
+    loads = jnp.sum(
+        jnp.where(
+            free[:, :, None],
+            until((start + beyond)[:, None, :], rank[:, :, None])
+            - until(start[:, None, :], rank[:, :, None]),
+            0,
+        ),
+        axis=0,
+    )
+    fits = jnp.all(total <= ROUND_ONE * relays) & jnp.all(loads <= ROUND_TWO)
+
+    turn = pick(rank)
+    serves = pick(free.astype(jnp.int32)) > 0
+    begin = until(start, turn[:, None])
+    passed = jnp.where(serves[:, None], until(start + beyond, turn[:, None]) - begin, 0)
+    shifted = line[None, :] * ROUND_TWO + above(passed) - begin
+    depth = jnp.arange(64, dtype=jnp.int32)
+    ordinal = depth[None, :] * relays + turn[:, None]
+    inside = (ordinal[:, :, None] >= start[:, None, :]) & (
+        ordinal[:, :, None] < (start + beyond)[:, None, :]
+    )
+    dest = jnp.sum(jnp.where(inside, shifted[:, None, :], 0), axis=2) + depth[None, :]
+    limit = blocks * ROUND_TWO
+    good = serves[:, None] & (ordinal < total[:, None]) & (depth < ROUND_ONE)[None, :]
+    dest = jnp.where(good, jnp.clip(dest, 0, limit - 1), limit)
+    held = jnp.where(serves, jnp.clip(until(total, turn), 0, ROUND_ONE), 0)
+
+    mine_start = pick(start)
+    mine_beyond = pick(beyond)
+    begin = until(mine_start[:, None], rank)
+    passed = jnp.where(free, until((mine_start + mine_beyond)[:, None], rank) - begin, 0)
+    shifted = line[None, :] * ROUND_TWO + above(passed) - begin
+    entry = jnp.arange(128, dtype=jnp.int32)
+    ordinal = mine_start[:, None] + entry[None, :]
+    chosen = free[:, None, :] & (rank[:, None, :] == (ordinal & (relays - 1))[:, :, None])
+    places = jnp.sum(jnp.where(chosen, shifted[:, None, :], 0), axis=2) + (ordinal >> shift)
+    places = jnp.where(
+        entry[None, :] < mine_beyond[:, None], jnp.clip(places, 0, limit - 1), 0
+    )
+    return fits, held, dest, mine_beyond, places
+
+
 def local(
     hidden_in,
     qkv_weight,
@@ -369,7 +845,7 @@
     slot_index = jnp.arange(KEPT, dtype=jnp.int32)
     take = lambda array: lax.dynamic_slice_in_dim(array, first, rows_here, 0)
 
-    outgoing = pack(
+    source_arguments = (
         block_index,
         page_table,
         request_lengths,
@@ -380,8 +856,16 @@
         cache_pool,
         blocks,
     )
-    outgoing = outgoing.reshape(blocks, ROWS, HEAD_DIM)
-    arrived = lax.all_to_all(outgoing, "blk", split_axis=0, concat_axis=0, tiled=True)
+
+    def exchange(rows):
+        return lax.all_to_all(
+            rows.reshape(blocks, -1, HEAD_DIM), "blk", split_axis=0, concat_axis=0, tiled=True
+        )
+
+    direct = exchange(spread(*source_arguments)).reshape(-1, LANES, HEAD_DIM)
+    fits, held, dest, beyond, places = routes(
+        request_order, retained_counts, block_index, blocks, rows_here
+    )
 
     old_ids = take(request_order)
     sources = old_ids // rows_here
@@ -412,6 +896,11 @@
     bias = jnp.pad(bias, ((0, 0), (0, 0), (0, PAD_ROWS - ROWS)), constant_values=NEG)
 
     gathered = lax.all_gather(hidden_in, "head", axis=1, tiled=True)
+    held, dest, beyond, places, sources, bias, fits, gathered = lax.optimization_barrier(
+        (held, dest, beyond, places, sources, bias, fits, gathered)
+    )
+    relayed = exchange(forward_rows(held, dest, direct, blocks)).reshape(-1, LANES, HEAD_DIM)
+
     normed = layer_norm(gathered.astype(jnp.float32)).astype(jnp.bfloat16)
     project = lambda index: jnp.dot(
         normed, qkv_weight[:, index], preferred_element_type=jnp.float32
@@ -423,17 +912,40 @@
     new_keys = pad_heads(rotate(project(1), lengths))
     new_values = pad_heads(project(2))
 
-    packed, share = attend(
-        sources, queries, new_keys, new_values, bias, out_weight, arrived, peers
-    )
+    def whole_shape(packed):
+        return (
+            packed.reshape(rows_here, SLOTS, heads_here, 2, HEAD_DIM)
+            .transpose(0, 1, 3, 2, 4)
+            .reshape(rows_here, SLOTS, 2, head_width)
+        )
+
+    def two_rounds():
+        packed, share = gather_attend(
+            sources,
+            beyond,
+            places,
+            queries,
+            new_keys,
+            new_values,
+            bias,
+            out_weight,
+            direct,
+            relayed,
+            peers,
+        )
+        return whole_shape(packed), share
+
+    def one_round():
+        arrived = exchange(pack(*source_arguments))
+        packed, share = attend(
+            sources, queries, new_keys, new_values, bias, out_weight, arrived, peers
+        )
+        return whole_shape(packed), share
+
+    packed_cache, share = lax.cond(fits, two_rounds, one_round)
     parts = lax.all_to_all(share, "head", split_axis=0, concat_axis=0, tiled=True)
     summed = jnp.sum(parts.astype(jnp.float32), axis=0)
     hidden_out = (hidden_in.astype(jnp.float32) + summed).astype(jnp.bfloat16)
-    packed_cache = (
-        packed.reshape(rows_here, SLOTS, heads_here, 2, HEAD_DIM)
-        .transpose(0, 1, 3, 2, 4)
-        .reshape(rows_here, SLOTS, 2, head_width)
-    )
     return (hidden_out, packed_cache)
 
 

time: 137 us -> 123 us (0.90)
  waiting for transfers between devices: 62.8 us -> 27.5 us
  starting transfers between devices: 12.2 us -> 18.7 us
  Pallas kernels: 13.4 us -> 18.7 us
  other arithmetic: 4.1 us -> 7.79 us
  local copies, waits for them, and re-layouts: 12.4 us -> 15.6 us
  between operations: 0.86 us -> 2.32 us
    all_to_all x1 -> x2, waiting for transfers between devices: 62.8 us -> 27.5 us  [exchange(): lax.all_to_all(rows.reshape(blocks, -1, HEAD_DIM), 'blk', split_axis=0, c...]
    all_to_all x1 -> x2, starting transfers between devices: 12.2 us -> 18.7 us  [exchange(): lax.all_to_all(rows.reshape(blocks, -1, HEAD_DIM), 'blk', split_axis=0, c...]
    pallas_call x2 -> x3, Pallas kernels: 13.4 us -> 18.7 us  [the longest x1 9.19 us: spread(): pl.pallas_call(spread_kernel, out_shape=pltpu.HBM((blocks * ROUND_ONE, LA...]
    dot_general x5 -> x4, local copies, waits for them, and re-layouts: 6.54 us -> 10.5 us  [local(): jnp.dot(normed, qkv_weight[:, index], preferred_element_type=jnp.float32)]
    reduce_sum x0 -> x8, other arithmetic: none -> 3.5 us  [the longest x1 1.15 us: routes(): jnp.sum(jnp.where(lower[None], array[:, None, :], 0), axis=2)]
    reduce_and x0 -> x2, other arithmetic: none -> 1.38 us  [routes(): fits = jnp.all(total <= ROUND_ONE * relays) & jnp.all(loads <= ROUND_TWO)]
  transfers between devices with their start and end apart: 1 -> 2, of which waited for: 1 -> 2; matrix products, arithmetic and copies ran while one was open for 14% -> 22% of each run, Pallas kernels for 0% -> 0%
where the time goes in v4:
time: 123 us; the launch traced here: 122 us
  blocking collectives  27.8 us (23%)
  waiting for transfers between devices  27.5 us (22%)
  Pallas kernels  18.7 us (15%)
  starting transfers between devices  18.7 us (15%)
  local copies, waits for them, and re-layouts  15.6 us (13%)
  other arithmetic  7.79 us (6%)
  matrix products  3.6 us (3%)
  between operations  2.32 us (2%)
    all_to_all x2, waiting for transfers between devices, exchange(): lax.all_to_all(rows.reshape(blocks, -1, HEAD_DIM), 'blk', split_axis=0, c...  27.5 us
    all_to_all x2, starting transfers between devices, exchange(): lax.all_to_all(rows.reshape(blocks, -1, HEAD_DIM), 'blk', split_axis=0, c...  18.7 us
    all_to_all x1, blocking collectives, local(): lax.all_to_all(share, 'head', split_axis=0, concat_axis=0, tiled=True)  13.9 us
    all_gather x1, blocking collectives, local(): gathered = lax.all_gather(hidden_in, 'head', axis=1, tiled=True)  13.9 us
    dot_general x4, local copies, waits for them, and re-layouts, local(): jnp.dot(normed, qkv_weight[:, index], preferred_element_type=jnp.float32)  10.5 us
    pallas_call x1, Pallas kernels, spread(): pl.pallas_call(spread_kernel, out_shape=pltpu.HBM((blocks * ROUND_ONE, LA...  9.19 us
    pallas_call x1, Pallas kernels, gather_attend(): pl.pallas_call(gather_attend_kernel, out_shape=(pltpu.HBM((count * SLOTS,...  5.84 us
    pallas_call x1, Pallas kernels, forward_rows(): pl.pallas_call(relay_kernel, out_shape=pltpu.HBM((blocks * ROUND_TWO, LAN...  3.63 us
  transfers between devices with their start and end apart: 2, of which 2 were waited for; matrix products, arithmetic and copies ran while one was open for 22% of the time, Pallas kernels for 0%

profile of v4, /device:TPU:1, one launch (start us, length us, event | category | flops | bytes accessed | tf_op | source)
XLA Modules:
  0.0 122.1 jit_solution(9765627284819615792)
XLA Ops:
  0.6 9.2 %spread.1 = bf16[1728,4,128]{2,1,0:T(4,128)(2,1)} custom-call(s32[1]{0:T(128)} %bitcast.27.block_ref, s32[4,16]{1,0:T(4,128)} %bitcast.72, s32[512]{0:T(512)} %length_hbm.1, s32[512]{0:T(512)} %count_hbm.1, s32[4,128]{1,0:T(4,128)} %bitcast.70, s32[512,128]{1,0:T(8,128)} %keep_hbm.1, f32[512,256]{1,0:T(8,128)} %weight_hbm.1, bf16[4096,4,128]{2,1,0:T(4,128)(2,1)} %bitcast.57), custom_call_target="tpu_custom_call" | custom-call | tf_op jit(solution)/shard_map/spread/pallas_call | solution.py:544
  9.9 11.9 %all-to-all-start.1 = ((bf16[32,216,128]{2,1,0:T(8,128)(2,1)}), bf16[32,216,128]{2,1,0:T(8,128)(2,1)S(1)}, u32[]{:S(2)}, u32[]{:S(2)}) async-start(bf16[32,216,128]{2,1,0:T(8,128)(2,1)} %bitcast.63), calls=%async_computation.1 | async-start | bytes 3538944 | tf_op jit(solution)/shard_map/all_to_all | solution.py:861
  22.6 0.7 gather_fusion
  23.2 1.5 %gather_fusion.2 = s32[16,128]{1,0:T(8,128)S(1)} fusion(s32[512,128]{1,0:T(8,128)} %keep_hbm.1, s32[1024]{0:T(1024)S(1)} %pad_clamp_fusion), kind=kCustom, calls=%fused_computation.2 | custom fusion | bytes 16448 | tf_op jit(solution)/shard_map/gather | solution.py:874
  24.8 0.7 gather_fusion.1
  25.4 1.6 %gather_fusion.3 = f32[16,256]{1,0:T(8,128)S(1)} fusion(f32[512,256]{1,0:T(8,128)} %weight_hbm.1, s32[1024]{0:T(1024)S(1)} %pad_clamp_fusion), kind=kCustom, calls=%fused_computation.3 | custom fusion | bytes 32832 | tf_op jit(solution)/shard_map/gather | solution.py:879
  27.1 1.2 select_reduce_fusion.6
  30.1 0.7 compare_reduce_fusion.1
  30.7 0.7 compare_reduce_fusion
  33.0 13.9 %all_gather.3 = bf16[16,2048]{1,0:T(8,128)(2,1)S(1)} all-gather(bf16[16,256]{1,0:T(8,128)(2,1)S(1)} %copy-done.6), channel_id=1, replica_groups=mesh['head'=8,'blk'=32] {'head'}, dimensions={1}, use_global_device_ids=true | all-gather | bytes 73728 | tf_op jit(solution)/shard_map/all_gather | solution.py:898
  48.8 14.9 %all-to-all-done.1 = bf16[32,216,128]{2,1,0:T(8,128)(2,1)S(1)} async-done(((bf16[32,216,128]{2,1,0:T(8,128)(2,1)}), bf16[32,216,128]{2,1,0:T(8,128)(2,1)S(1)}, u32[]{:S(2)}, u32[]{:S(2)}) %all-to-all-start.1) | async-done | bytes 1769504 | tf_op jit(solution)/shard_map/all_to_all | solution.py:861
  63.7 3.6 %relay.1 = bf16[1152,4,128]{2,1,0:T(4,128)(2,1)} custom-call(s32[32]{0:T(128)S(1)} %clamp_select_fusion.2.held_ref, s32[32,64]{1,0:T(8,128)S(1)} %clamp_select_fusion.1.dest_ref, bf16[1728,4,128]{2,1,0:T(4,128)(2,1)S(1)} %bitcast.61), custom_call_target="tpu_custom_call" | custom-call | tf_op jit(solution)/shard_map/relay/pallas_call | solution.py:601
  67.3 6.8 %all-to-all-start.2 = ((bf16[32,144,128]{2,1,0:T(8,128)(2,1)}), bf16[32,144,128]{2,1,0:T(8,128)(2,1)S(1)}, u32[]{:S(2)}, u32[]{:S(2)}) async-start(bf16[32,144,128]{2,1,0:T(8,128)(2,1)} %bitcast.65), calls=%async_computation.2 | async-start | bytes 2359296 | tf_op jit(solution)/shard_map/all_to_all | solution.py:861
  74.1 3.6 %slice_bitcast_fusion = (bf16[256,2048]{0,1:T(8,128)(2,1)}, bf16[256,2048]{0,1:T(8,128)(2,1)}, bf16[256,2048]{0,1:T(8,128)(2,1)}) fusion(bf16[2048,3,256]{2,0,1:T(8,128)(2,1)} %param.13), kind=kLoop, calls=%fused_computation.7 | loop fusion | bytes 6291456 | tf_op jit(solution)/shard_map/dot_general | solution.py:905
  77.7 2.3 %copy.41 = bf16[256,2048]{1,0:T(8,128)(2,1)} copy(bf16[256,2048]{0,1:T(8,128)(2,1)} %get-tuple-element.184) | data formatting | bytes 2097152 | tf_op jit(solution)/shard_map/dot_general | solution.py:905
  80.0 2.3 %copy.39 = bf16[256,2048]{1,0:T(8,128)(2,1)} copy(bf16[256,2048]{0,1:T(8,128)(2,1)} %get-tuple-element.185) | data formatting | bytes 2097152 | tf_op jit(solution)/shard_map/dot_general | solution.py:905
  82.3 2.3 %copy.40 = bf16[256,2048]{1,0:T(8,128)(2,1)} copy(bf16[256,2048]{0,1:T(8,128)(2,1)} %get-tuple-element.186) | data formatting | bytes 2097152 | tf_op jit(solution)/shard_map/dot_general | solution.py:905
  84.9 1.6 %convolution_convert_fusion = bf16[16,2,128]{2,0,1:T(8,128)(2,1)S(1)} fusion(bf16[2,128,2048]{2,1,0:T(8,128)(2,1)} %bitcast.68, bf16[16,2048]{1,0:T(8,128)(2,1)S(1)} %all_gather.3, f32[16]{0:T(128)S(1)} %add_rsqrt_fusion, f32[16]{0:T(128)S(1)} %broadcast_multiply_fusion), kind=kOutput, calls=%fused_computation.6 | convolution fusion | flops 16912384 | bytes 1122432 | tf_op jit(solution)/shard_map/dot_general | solution.py:905
  86.7 1.6 %fusion.21 = f32[16,2,128]{2,0,1:T(8,128)S(1)} fusion(bf16[2,128,2048]{2,1,0:T(8,128)(2,1)} %bitcast.66, bf16[16,2048]{1,0:T(8,128)(2,1)S(1)} %all_gather.3, f32[16]{0:T(128)S(1)} %add_rsqrt_fusion, f32[16]{0:T(128)S(1)} %broadcast_multiply_fusion), kind=kOutput, calls=%fused_computation.82 | convolution fusion | flops 16908288 | bytes 1130624 | tf_op jit(solution)/shard_map/dot_general | solution.py:905
  89.0 12.7 %all-to-all-done.2 = bf16[32,144,128]{2,1,0:T(8,128)(2,1)S(1)} async-done(((bf16[32,144,128]{2,1,0:T(8,128)(2,1)}), bf16[32,144,128]{2,1,0:T(8,128)(2,1)S(1)}, u32[]{:S(2)}, u32[]{:S(2)}) %all-to-all-start.2) | async-done | bytes 1179680 | tf_op jit(solution)/shard_map/all_to_all | solution.py:861
  101.6 5.9 %conditional.1 = (bf16[16,132,2,256]{3,2,1,0:T(2,128)(2,1)}, bf16[8,16,256]{2,1,0:T(8,128)(2,1)S(1)}) conditional(s32[]{:T(128)} %convert_element_type.45, (s32[]{:T(128)}, s32[16,4]{0,1:T(4,128)}, s32[512]{0:T(512)S(1)}, bf16[64,64,2,256]{3,2,1,0:T(2,128)(2,1)}, s32[512]{0:T(512)S(1)}, /*index=5*/s32[512]{0:T(512)S(1)}, s32[512,128]{1,0:T(8,128)}, ...), branch_computations={%region_20.21_spmd, %region_21.22_spmd} | conditional | bytes 17391776 | solution.py:945
  101.7 5.8 %gather_attend.1 = (bf16[2112,4,128]{2,1,0:T(4,128)(2,1)}, bf16[8,16,256]{2,1,0:T(8,128)(2,1)S(1)}) custom-call(s32[16]{0:T(128)S(1)} %get-tuple-element.65.source_ref, s32[32]{0:T(128)S(1)} %get-tuple-element.66.beyond_ref, s32[32,128]{1,0:T(8,128)S(1)} %get-tuple-element.67.place_ref, bf16[16,8,128]{2,1,0:T(8,128)(2,1)S(1)} %copy.46.query_ref, ...), custom_call_target="tpu_custom_call" | custom-call | tf_op jit(solution)/shard_map/cond/branch_1_fun/gather_attend/pallas_call | solution.py:727
  107.5 13.9 %all_to_all.19 = bf16[8,16,256]{2,1,0:T(8,128)(2,1)S(1)} all-to-all(bf16[8,16,256]{2,1,0:T(8,128)(2,1)S(1)} %get-tuple-element.97), channel_id=1, replica_groups=mesh['head'=8,'blk'=32] {'head'}, dimensions={0} | all-to-all | bytes 131072 | tf_op jit(solution)/shard_map/all_to_all | solution.py:946
  121.5 0.6 add_convert_fusion
  (74 shorter events, 5.7 us)
Async XLA Ops:
  9.8 12.0 %copy-start = (s32[512]{0:T(512)S(1)}, s32[512]{0:T(512)}, u32[]{:S(2)}) copy-start(s32[512]{0:T(512)} %count_hbm.1) | copy-start | bytes 6148
  9.8 12.0 %copy-start.7 = (s32[512]{0:T(512)S(1)}, s32[512]{0:T(512)}, u32[]{:S(2)}) copy-start(s32[512]{0:T(512)} %param.17) | copy-start | bytes 6148
  9.9 14.9 %copy-start.2 = (s32[512]{0:T(512)S(1)}, s32[512]{0:T(512)}, u32[]{:S(2)}) copy-start(s32[512]{0:T(512)} %length_hbm.1) | copy-start | bytes 6148
  9.9 53.8 %all-to-all-start.1 = ((bf16[32,216,128]{2,1,0:T(8,128)(2,1)}), bf16[32,216,128]{2,1,0:T(8,128)(2,1)S(1)}, u32[]{:S(2)}, u32[]{:S(2)}) async-start(bf16[32,216,128]{2,1,0:T(8,128)(2,1)} %bitcast.63), calls=%async_computation.1 | async-start | bytes 3538944 | tf_op jit(solution)/shard_map/all_to_all | solution.py:861
  21.8 11.2 %copy-start.6 = (bf16[16,256]{1,0:T(8,128)(2,1)S(1)}, bf16[16,256]{1,0:T(8,128)(2,1)}, u32[]{:S(2)}) copy-start(bf16[16,256]{1,0:T(8,128)(2,1)} %param.12) | copy-start | bytes 24580
  67.3 34.3 %all-to-all-start.2 = ((bf16[32,144,128]{2,1,0:T(8,128)(2,1)}), bf16[32,144,128]{2,1,0:T(8,128)(2,1)S(1)}, u32[]{:S(2)}, u32[]{:S(2)}) async-start(bf16[32,144,128]{2,1,0:T(8,128)(2,1)} %bitcast.65), calls=%async_computation.2 | async-start | bytes 2359296 | tf_op jit(solution)/shard_map/all_to_all | solution.py:861
  84.6 3.7 %copy-start.4 = (bf16[256,2048]{1,0:T(8,128)(2,1)S(1)}, bf16[256,2048]{1,0:T(8,128)(2,1)}, u32[]{:S(2)}) copy-start(bf16[256,2048]{1,0:T(8,128)(2,1)} %copy.40) | copy-start | bytes 3145732

commit v5 on v4

--- a/solution.py
+++ b/solution.py
@@ -1,3 +1,5 @@
+import functools
+
 import jax
 import jax.numpy as jnp
 from jax import lax
@@ -495,15 +497,25 @@
     move_spots.wait()
     move_dests.wait()
     load_rows.wait()
+    straight = (ROUND_ONE - PAGES) // group
     for i in range(count):
-
-        def gather(c, carry):
+        slot = targets[i] * ROUND_ONE + PAGES
+        full = (count_smem[first + i] + group - 1) >> 4
+
+        def gather(c):
+            picked = [rows_vmem[spot_smem[i, c * group + u]] for u in range(group)]
+            for u in range(group):
+                out_vmem[slot + c * group + u] = picked[u]
+
+        def scatter(c):
             picked = [rows_vmem[spot_smem[i, c * group + u]] for u in range(group)]
             for u in range(group):
                 out_vmem[dest_smem[i, c * group + u]] = picked[u]
-            return carry
-
-        lax.fori_loop(0, (count_smem[first + i] + group - 1) >> 4, gather, 0)
+
+        for c in range(straight):
+            gather(c)
+        for c in range(straight, KEPT // group):
+            pl.when(c < full)(functools.partial(scatter, c))
 
     flat = rows_vmem.reshape(rows_vmem.shape[0] * LANES, HEAD_DIM)
     for i in range(count):
@@ -580,18 +592,22 @@
 def relay_kernel(held_ref, dest_ref, recv_ref, send_hbm, out_vmem, out_sem):
     slots = held_ref.shape[0]
 
-    def source(s, carry):
-        def forward(c, inner):
+    for s in range(slots):
+        held = held_ref[s]
+
+        def forward(c):
             start = s * ROUND_ONE + c * STEP
             picked = [recv_ref[start + u] for u in range(STEP)]
             for u in range(STEP):
                 out_vmem[dest_ref[s, c * STEP + u]] = picked[u]
-            return inner
-
-        lax.fori_loop(0, lax.div(held_ref[s] + (STEP - 1), STEP), forward, 0)
-        return carry
-
-    lax.fori_loop(0, slots, source, 0)
+
+        @pl.when(held > 0)
+        def _():
+            for c in range(3):
+                forward(c)
+            for c in range(3, ROUND_ONE // STEP):
+                pl.when(c * STEP < held)(functools.partial(forward, c))
+
     out = pltpu.make_async_copy(out_vmem.at[pl.ds(0, slots * ROUND_TWO)], send_hbm, out_sem)
     out.start()
     out.wait()
@@ -667,16 +683,16 @@
         rows_vmem[pl.ds(r * SLOTS, head)] = direct_ref[pl.ds(start + PAGES, head)]
         rows_vmem[pl.ds(r * SLOTS + KEPT, PAGES)] = direct_ref[pl.ds(start, PAGES)]
 
-        def place(c, carry):
+        def place(c):
             picked = [relayed_ref[place_ref[source, c * STEP + u]] for u in range(STEP)]
             for u in range(STEP):
                 past = c * STEP + u >= beyond
                 rows_vmem[r * SLOTS + head + c * STEP + u] = jnp.where(
                     past, zero_rows[0], picked[u]
                 )
-            return carry
-
-        lax.fori_loop(0, lax.div(beyond + (STEP - 1), STEP), place, 0)
+
+        for c in range((KEPT - head) // STEP):
+            pl.when(c * STEP < beyond)(functools.partial(place, c))
         outs[r].start()
     flat = rows_vmem.reshape(rows_vmem.shape[0] * LANES, HEAD_DIM)
     for r in range(count):

time: 123 us -> 120 us (0.976)
  Pallas kernels: 18.7 us -> 15.8 us
    pallas_call x1, Pallas kernels: 9.19 us -> 6.58 us  [spread(): pl.pallas_call(spread_kernel, out_shape=pltpu.HBM((blocks * ROUND_ONE, LA...]
where the time goes in v5:
time: 120 us; the launch traced here: 119 us
  blocking collectives  27.7 us (23%)
  waiting for transfers between devices  27.6 us (23%)
  starting transfers between devices  18.8 us (16%)
  Pallas kernels  15.8 us (13%)
  local copies, waits for them, and re-layouts  15.6 us (13%)
  other arithmetic  7.79 us (6%)
  matrix products  3.6 us (3%)
  between operations  2.32 us (2%)
    all_to_all x2, waiting for transfers between devices, exchange(): lax.all_to_all(rows.reshape(blocks, -1, HEAD_DIM), 'blk', split_axis=0, c...  27.6 us
    all_to_all x2, starting transfers between devices, exchange(): lax.all_to_all(rows.reshape(blocks, -1, HEAD_DIM), 'blk', split_axis=0, c...  18.8 us
    all_gather x1, blocking collectives, local(): gathered = lax.all_gather(hidden_in, 'head', axis=1, tiled=True)  13.9 us
    all_to_all x1, blocking collectives, local(): lax.all_to_all(share, 'head', split_axis=0, concat_axis=0, tiled=True)  13.8 us
    dot_general x4, local copies, waits for them, and re-layouts, local(): jnp.dot(normed, qkv_weight[:, index], preferred_element_type=jnp.float32)  10.5 us
    pallas_call x1, Pallas kernels, spread(): pl.pallas_call(spread_kernel, out_shape=pltpu.HBM((blocks * ROUND_ONE, LA...  6.58 us
    pallas_call x1, Pallas kernels, gather_attend(): pl.pallas_call(gather_attend_kernel, out_shape=(pltpu.HBM((count * SLOTS,...  6.41 us
    dot_general x3, matrix products, local(): jnp.dot(normed, qkv_weight[:, index], preferred_element_type=jnp.float32)  3.6 us
  transfers between devices with their start and end apart: 2, of which 2 were waited for; matrix products, arithmetic and copies ran while one was open for 22% of the time, Pallas kernels for 0%

profile of v5, /device:TPU:1, one launch (start us, length us, event | category | flops | bytes accessed | tf_op | source)
XLA Modules:
  0.0 119.3 jit_solution(10356816843376809270)
XLA Ops:
  0.6 6.6 %spread.1 = bf16[1728,4,128]{2,1,0:T(4,128)(2,1)} custom-call(s32[1]{0:T(128)} %bitcast.27.block_ref, s32[4,16]{1,0:T(4,128)} %bitcast.72, s32[512]{0:T(512)} %length_hbm.1, s32[512]{0:T(512)} %count_hbm.1, s32[4,128]{1,0:T(4,128)} %bitcast.70, s32[512,128]{1,0:T(8,128)} %keep_hbm.1, f32[512,256]{1,0:T(8,128)} %weight_hbm.1, bf16[4096,4,128]{2,1,0:T(4,128)(2,1)} %bitcast.57), custom_call_target="tpu_custom_call" | custom-call | tf_op jit(solution)/shard_map/spread/pallas_call | solution.py:556
  7.3 12.0 %all-to-all-start.1 = ((bf16[32,216,128]{2,1,0:T(8,128)(2,1)}), bf16[32,216,128]{2,1,0:T(8,128)(2,1)S(1)}, u32[]{:S(2)}, u32[]{:S(2)}) async-start(bf16[32,216,128]{2,1,0:T(8,128)(2,1)} %bitcast.63), calls=%async_computation.1 | async-start | bytes 3538944 | tf_op jit(solution)/shard_map/all_to_all | solution.py:877
  20.0 0.7 gather_fusion
  20.7 1.5 %gather_fusion.2 = s32[16,128]{1,0:T(8,128)S(1)} fusion(s32[512,128]{1,0:T(8,128)} %keep_hbm.1, s32[1024]{0:T(1024)S(1)} %pad_clamp_fusion), kind=kCustom, calls=%fused_computation.2 | custom fusion | bytes 16448 | tf_op jit(solution)/shard_map/gather | solution.py:890
  22.2 0.7 gather_fusion.1
  22.9 1.6 %gather_fusion.3 = f32[16,256]{1,0:T(8,128)S(1)} fusion(f32[512,256]{1,0:T(8,128)} %weight_hbm.1, s32[1024]{0:T(1024)S(1)} %pad_clamp_fusion), kind=kCustom, calls=%fused_computation.3 | custom fusion | bytes 32832 | tf_op jit(solution)/shard_map/gather | solution.py:895
  24.5 1.2 select_reduce_fusion.6
  27.5 0.7 compare_reduce_fusion.1
  28.1 0.7 compare_reduce_fusion
  30.4 13.9 %all_gather.3 = bf16[16,2048]{1,0:T(8,128)(2,1)S(1)} all-gather(bf16[16,256]{1,0:T(8,128)(2,1)S(1)} %copy-done.6), channel_id=1, replica_groups=mesh['head'=8,'blk'=32] {'head'}, dimensions={1}, use_global_device_ids=true | all-gather | bytes 73728 | tf_op jit(solution)/shard_map/all_gather | solution.py:914
  46.2 14.9 %all-to-all-done.1 = bf16[32,216,128]{2,1,0:T(8,128)(2,1)S(1)} async-done(((bf16[32,216,128]{2,1,0:T(8,128)(2,1)}), bf16[32,216,128]{2,1,0:T(8,128)(2,1)S(1)}, u32[]{:S(2)}, u32[]{:S(2)}) %all-to-all-start.1) | async-done | bytes 1769504 | tf_op jit(solution)/shard_map/all_to_all | solution.py:877
  61.1 2.9 %relay.1 = bf16[1152,4,128]{2,1,0:T(4,128)(2,1)} custom-call(s32[32]{0:T(128)S(1)} %clamp_select_fusion.2.held_ref, s32[32,64]{1,0:T(8,128)S(1)} %clamp_select_fusion.1.dest_ref, bf16[1728,4,128]{2,1,0:T(4,128)(2,1)S(1)} %bitcast.61), custom_call_target="tpu_custom_call" | custom-call | tf_op jit(solution)/shard_map/relay/pallas_call | solution.py:617
  63.9 6.8 %all-to-all-start.2 = ((bf16[32,144,128]{2,1,0:T(8,128)(2,1)}), bf16[32,144,128]{2,1,0:T(8,128)(2,1)S(1)}, u32[]{:S(2)}, u32[]{:S(2)}) async-start(bf16[32,144,128]{2,1,0:T(8,128)(2,1)} %bitcast.65), calls=%async_computation.2 | async-start | bytes 2359296 | tf_op jit(solution)/shard_map/all_to_all | solution.py:877
  70.8 3.6 %slice_bitcast_fusion = (bf16[256,2048]{0,1:T(8,128)(2,1)}, bf16[256,2048]{0,1:T(8,128)(2,1)}, bf16[256,2048]{0,1:T(8,128)(2,1)}) fusion(bf16[2048,3,256]{2,0,1:T(8,128)(2,1)} %param.13), kind=kLoop, calls=%fused_computation.7 | loop fusion | bytes 6291456 | tf_op jit(solution)/shard_map/dot_general | solution.py:921
  74.4 2.3 %copy.41 = bf16[256,2048]{1,0:T(8,128)(2,1)} copy(bf16[256,2048]{0,1:T(8,128)(2,1)} %get-tuple-element.184) | data formatting | bytes 2097152 | tf_op jit(solution)/shard_map/dot_general | solution.py:921
  76.7 2.3 %copy.39 = bf16[256,2048]{1,0:T(8,128)(2,1)} copy(bf16[256,2048]{0,1:T(8,128)(2,1)} %get-tuple-element.185) | data formatting | bytes 2097152 | tf_op jit(solution)/shard_map/dot_general | solution.py:921
  78.9 2.3 %copy.40 = bf16[256,2048]{1,0:T(8,128)(2,1)} copy(bf16[256,2048]{0,1:T(8,128)(2,1)} %get-tuple-element.186) | data formatting | bytes 2097152 | tf_op jit(solution)/shard_map/dot_general | solution.py:921
  81.6 1.6 %convolution_convert_fusion = bf16[16,2,128]{2,0,1:T(8,128)(2,1)S(1)} fusion(bf16[2,128,2048]{2,1,0:T(8,128)(2,1)} %bitcast.68, bf16[16,2048]{1,0:T(8,128)(2,1)S(1)} %all_gather.3, f32[16]{0:T(128)S(1)} %add_rsqrt_fusion, f32[16]{0:T(128)S(1)} %broadcast_multiply_fusion), kind=kOutput, calls=%fused_computation.6 | convolution fusion | flops 16912384 | bytes 1122432 | tf_op jit(solution)/shard_map/dot_general | solution.py:921
  83.3 1.6 %fusion.21 = f32[16,2,128]{2,0,1:T(8,128)S(1)} fusion(bf16[2,128,2048]{2,1,0:T(8,128)(2,1)} %bitcast.66, bf16[16,2048]{1,0:T(8,128)(2,1)S(1)} %all_gather.3, f32[16]{0:T(128)S(1)} %add_rsqrt_fusion, f32[16]{0:T(128)S(1)} %broadcast_multiply_fusion), kind=kOutput, calls=%fused_computation.82 | convolution fusion | flops 16908288 | bytes 1130624 | tf_op jit(solution)/shard_map/dot_general | solution.py:921
  85.6 12.7 %all-to-all-done.2 = bf16[32,144,128]{2,1,0:T(8,128)(2,1)S(1)} async-done(((bf16[32,144,128]{2,1,0:T(8,128)(2,1)}), bf16[32,144,128]{2,1,0:T(8,128)(2,1)S(1)}, u32[]{:S(2)}, u32[]{:S(2)}) %all-to-all-start.2) | async-done | bytes 1179680 | tf_op jit(solution)/shard_map/all_to_all | solution.py:877
  98.3 6.5 %conditional.1 = (bf16[16,132,2,256]{3,2,1,0:T(2,128)(2,1)}, bf16[8,16,256]{2,1,0:T(8,128)(2,1)S(1)}) conditional(s32[]{:T(128)} %convert_element_type.45, (s32[]{:T(128)}, s32[16,4]{0,1:T(4,128)}, s32[512]{0:T(512)S(1)}, bf16[64,64,2,256]{3,2,1,0:T(2,128)(2,1)}, s32[512]{0:T(512)S(1)}, /*index=5*/s32[512]{0:T(512)S(1)}, s32[512,128]{1,0:T(8,128)}, ...), branch_computations={%region_20.21_spmd, %region_21.22_spmd} | conditional | bytes 17391776 | solution.py:961
  98.4 6.4 %gather_attend.1 = (bf16[2112,4,128]{2,1,0:T(4,128)(2,1)}, bf16[8,16,256]{2,1,0:T(8,128)(2,1)S(1)}) custom-call(s32[16]{0:T(128)S(1)} %get-tuple-element.65.source_ref, s32[32]{0:T(128)S(1)} %get-tuple-element.66.beyond_ref, s32[32,128]{1,0:T(8,128)S(1)} %get-tuple-element.67.place_ref, bf16[16,8,128]{2,1,0:T(8,128)(2,1)S(1)} %copy.46.query_ref, ...), custom_call_target="tpu_custom_call" | custom-call | tf_op jit(solution)/shard_map/cond/branch_1_fun/gather_attend/pallas_call | solution.py:743
  104.8 13.8 %all_to_all.19 = bf16[8,16,256]{2,1,0:T(8,128)(2,1)S(1)} all-to-all(bf16[8,16,256]{2,1,0:T(8,128)(2,1)S(1)} %get-tuple-element.97), channel_id=1, replica_groups=mesh['head'=8,'blk'=32] {'head'}, dimensions={0} | all-to-all | bytes 131072 | tf_op jit(solution)/shard_map/all_to_all | solution.py:962
  118.7 0.6 add_convert_fusion
  (74 shorter events, 5.7 us)
Async XLA Ops:
  7.2 12.0 %copy-start = (s32[512]{0:T(512)S(1)}, s32[512]{0:T(512)}, u32[]{:S(2)}) copy-start(s32[512]{0:T(512)} %count_hbm.1) | copy-start | bytes 6148
  7.2 12.0 %copy-start.7 = (s32[512]{0:T(512)S(1)}, s32[512]{0:T(512)}, u32[]{:S(2)}) copy-start(s32[512]{0:T(512)} %param.17) | copy-start | bytes 6148
  7.2 14.9 %copy-start.2 = (s32[512]{0:T(512)S(1)}, s32[512]{0:T(512)}, u32[]{:S(2)}) copy-start(s32[512]{0:T(512)} %length_hbm.1) | copy-start | bytes 6148
  7.3 53.8 %all-to-all-start.1 = ((bf16[32,216,128]{2,1,0:T(8,128)(2,1)}), bf16[32,216,128]{2,1,0:T(8,128)(2,1)S(1)}, u32[]{:S(2)}, u32[]{:S(2)}) async-start(bf16[32,216,128]{2,1,0:T(8,128)(2,1)} %bitcast.63), calls=%async_computation.1 | async-start | bytes 3538944 | tf_op jit(solution)/shard_map/all_to_all | solution.py:877
  19.2 11.2 %copy-start.6 = (bf16[16,256]{1,0:T(8,128)(2,1)S(1)}, bf16[16,256]{1,0:T(8,128)(2,1)}, u32[]{:S(2)}) copy-start(bf16[16,256]{1,0:T(8,128)(2,1)} %param.12) | copy-start | bytes 24580
  63.9 34.4 %all-to-all-start.2 = ((bf16[32,144,128]{2,1,0:T(8,128)(2,1)}), bf16[32,144,128]{2,1,0:T(8,128)(2,1)S(1)}, u32[]{:S(2)}, u32[]{:S(2)}) async-start(bf16[32,144,128]{2,1,0:T(8,128)(2,1)} %bitcast.65), calls=%async_computation.2 | async-start | bytes 2359296 | tf_op jit(solution)/shard_map/all_to_all | solution.py:877
  81.2 3.7 %copy-start.4 = (bf16[256,2048]{1,0:T(8,128)(2,1)S(1)}, bf16[256,2048]{1,0:T(8,128)(2,1)}, u32[]{:S(2)}) copy-start(bf16[256,2048]{1,0:T(8,128)(2,1)} %copy.40) | copy-start | bytes 3145732

commit v6 on v5

--- a/solution.py
+++ b/solution.py
@@ -19,7 +19,7 @@
 PAD_ROWS = 640
 NEG = -1e30
 ROUND_ONE = 54
-ROUND_TWO = 36
+ROUND_TWO = 34
 STEP = 6
 
 epsilon = 1e-05

time: 120 us -> 119 us (level)
  waiting for transfers between devices: 27.6 us -> 26 us
    all_to_all x2, waiting for transfers between devices: 27.6 us -> 26 us  [exchange(): lax.all_to_all(rows.reshape(blocks, -1, HEAD_DIM), 'blk', split_axis=0, c...]
where the time goes in v6:
time: 119 us; the launch traced here: 118 us
  blocking collectives  27.9 us (23%)
  waiting for transfers between devices  26 us (22%)
  starting transfers between devices  19.2 us (16%)
  Pallas kernels  15.6 us (13%)
  local copies, waits for them, and re-layouts  15.6 us (13%)
  other arithmetic  7.78 us (7%)
  matrix products  3.69 us (3%)
  between operations  2.33 us (2%)
    all_to_all x2, waiting for transfers between devices, exchange(): lax.all_to_all(rows.reshape(blocks, -1, HEAD_DIM), 'blk', split_axis=0, c...  26 us
    all_to_all x2, starting transfers between devices, exchange(): lax.all_to_all(rows.reshape(blocks, -1, HEAD_DIM), 'blk', split_axis=0, c...  19.2 us
    all_to_all x1, blocking collectives, local(): lax.all_to_all(share, 'head', split_axis=0, concat_axis=0, tiled=True)  14 us
    all_gather x1, blocking collectives, local(): gathered = lax.all_gather(hidden_in, 'head', axis=1, tiled=True)  13.9 us
    dot_general x4, local copies, waits for them, and re-layouts, local(): jnp.dot(normed, qkv_weight[:, index], preferred_element_type=jnp.float32)  10.5 us
    pallas_call x1, Pallas kernels, gather_attend(): pl.pallas_call(gather_attend_kernel, out_shape=(pltpu.HBM((count * SLOTS,...  6.59 us
    pallas_call x1, Pallas kernels, spread(): pl.pallas_call(spread_kernel, out_shape=pltpu.HBM((blocks * ROUND_ONE, LA...  6.19 us
    dot_general x3, matrix products, local(): jnp.dot(normed, qkv_weight[:, index], preferred_element_type=jnp.float32)  3.69 us
  transfers between devices with their start and end apart: 2, of which 2 were waited for; matrix products, arithmetic and copies ran while one was open for 22% of the time, Pallas kernels for 0%

profile of v6, /device:TPU:1, one launch (start us, length us, event | category | flops | bytes accessed | tf_op | source)
XLA Modules:
  0.0 118.2 jit_solution(9768994753213376187)
XLA Ops:
  0.6 6.2 %spread.1 = bf16[1728,4,128]{2,1,0:T(4,128)(2,1)} custom-call(s32[1]{0:T(128)} %bitcast.27.block_ref, s32[4,16]{1,0:T(4,128)} %bitcast.72, s32[512]{0:T(512)} %length_hbm.1, s32[512]{0:T(512)} %count_hbm.1, s32[4,128]{1,0:T(4,128)} %bitcast.70, s32[512,128]{1,0:T(8,128)} %keep_hbm.1, f32[512,256]{1,0:T(8,128)} %weight_hbm.1, bf16[4096,4,128]{2,1,0:T(4,128)(2,1)} %bitcast.57), custom_call_target="tpu_custom_call" | custom-call | tf_op jit(solution)/shard_map/spread/pallas_call | solution.py:556
  6.9 12.3 %all-to-all-start.1 = ((bf16[32,216,128]{2,1,0:T(8,128)(2,1)}), bf16[32,216,128]{2,1,0:T(8,128)(2,1)S(1)}, u32[]{:S(2)}, u32[]{:S(2)}) async-start(bf16[32,216,128]{2,1,0:T(8,128)(2,1)} %bitcast.63), calls=%async_computation.1 | async-start | bytes 3538944 | tf_op jit(solution)/shard_map/all_to_all | solution.py:877
  19.9 0.7 gather_fusion
  20.6 1.5 %gather_fusion.2 = s32[16,128]{1,0:T(8,128)S(1)} fusion(s32[512,128]{1,0:T(8,128)} %keep_hbm.1, s32[1024]{0:T(1024)S(1)} %pad_clamp_fusion), kind=kCustom, calls=%fused_computation.2 | custom fusion | bytes 16448 | tf_op jit(solution)/shard_map/gather | solution.py:890
  22.1 0.7 gather_fusion.1
  22.8 1.6 %gather_fusion.3 = f32[16,256]{1,0:T(8,128)S(1)} fusion(f32[512,256]{1,0:T(8,128)} %weight_hbm.1, s32[1024]{0:T(1024)S(1)} %pad_clamp_fusion), kind=kCustom, calls=%fused_computation.3 | custom fusion | bytes 32832 | tf_op jit(solution)/shard_map/gather | solution.py:895
  24.5 1.2 select_reduce_fusion.6
  26.2 0.7 compare_reduce_fusion
  28.2 0.7 compare_reduce_fusion.1
  30.3 13.9 %all_gather.3 = bf16[16,2048]{1,0:T(8,128)(2,1)S(1)} all-gather(bf16[16,256]{1,0:T(8,128)(2,1)S(1)} %copy-done.6), channel_id=1, replica_groups=mesh['head'=8,'blk'=32] {'head'}, dimensions={1}, use_global_device_ids=true | all-gather | bytes 73728 | tf_op jit(solution)/shard_map/all_gather | solution.py:914
  46.1 3.6 %slice_bitcast_fusion = (bf16[256,2048]{0,1:T(8,128)(2,1)}, bf16[256,2048]{0,1:T(8,128)(2,1)}, bf16[256,2048]{0,1:T(8,128)(2,1)}) fusion(bf16[2048,3,256]{2,0,1:T(8,128)(2,1)} %param.13), kind=kLoop, calls=%fused_computation.7 | loop fusion | bytes 6291456 | tf_op jit(solution)/shard_map/dot_general | solution.py:921
  49.8 11.2 %all-to-all-done.1 = bf16[32,216,128]{2,1,0:T(8,128)(2,1)S(1)} async-done(((bf16[32,216,128]{2,1,0:T(8,128)(2,1)}), bf16[32,216,128]{2,1,0:T(8,128)(2,1)S(1)}, u32[]{:S(2)}, u32[]{:S(2)}) %all-to-all-start.1) | async-done | bytes 1769504 | tf_op jit(solution)/shard_map/all_to_all | solution.py:877
  61.0 2.8 %relay.1 = bf16[1088,4,128]{2,1,0:T(4,128)(2,1)} custom-call(s32[32]{0:T(128)S(1)} %clamp_select_fusion.2.held_ref, s32[32,64]{1,0:T(8,128)S(1)} %clamp_select_fusion.1.dest_ref, bf16[1728,4,128]{2,1,0:T(4,128)(2,1)S(1)} %bitcast.61), custom_call_target="tpu_custom_call" | custom-call | tf_op jit(solution)/shard_map/relay/pallas_call | solution.py:617
  63.8 7.0 %all-to-all-start.2 = ((bf16[32,136,128]{2,1,0:T(8,128)(2,1)}), bf16[32,136,128]{2,1,0:T(8,128)(2,1)S(1)}, u32[]{:S(2)}, u32[]{:S(2)}) async-start(bf16[32,136,128]{2,1,0:T(8,128)(2,1)} %bitcast.65), calls=%async_computation.2 | async-start | bytes 2228224 | tf_op jit(solution)/shard_map/all_to_all | solution.py:877
  71.0 2.3 %copy.41 = bf16[256,2048]{1,0:T(8,128)(2,1)} copy(bf16[256,2048]{0,1:T(8,128)(2,1)} %get-tuple-element.184) | data formatting | bytes 2097152 | tf_op jit(solution)/shard_map/dot_general | solution.py:921
  73.2 2.3 %copy.39 = bf16[256,2048]{1,0:T(8,128)(2,1)} copy(bf16[256,2048]{0,1:T(8,128)(2,1)} %get-tuple-element.185) | data formatting | bytes 2097152 | tf_op jit(solution)/shard_map/dot_general | solution.py:921
  75.5 2.3 %copy.40 = bf16[256,2048]{1,0:T(8,128)(2,1)} copy(bf16[256,2048]{0,1:T(8,128)(2,1)} %get-tuple-element.186) | data formatting | bytes 2097152 | tf_op jit(solution)/shard_map/dot_general | solution.py:921
  78.0 1.7 %convolution_convert_fusion = bf16[16,2,128]{2,0,1:T(8,128)(2,1)S(1)} fusion(bf16[2,128,2048]{2,1,0:T(8,128)(2,1)} %bitcast.68, bf16[16,2048]{1,0:T(8,128)(2,1)S(1)} %all_gather.3, f32[16]{0:T(128)S(1)} %add_rsqrt_fusion, f32[16]{0:T(128)S(1)} %broadcast_multiply_fusion), kind=kOutput, calls=%fused_computation.6 | convolution fusion | flops 16912384 | bytes 1122432 | tf_op jit(solution)/shard_map/dot_general | solution.py:921
  79.9 1.6 %fusion.21 = f32[16,2,128]{2,0,1:T(8,128)S(1)} fusion(bf16[2,128,2048]{2,1,0:T(8,128)(2,1)} %bitcast.66, bf16[16,2048]{1,0:T(8,128)(2,1)S(1)} %all_gather.3, f32[16]{0:T(128)S(1)} %add_rsqrt_fusion, f32[16]{0:T(128)S(1)} %broadcast_multiply_fusion), kind=kOutput, calls=%fused_computation.82 | convolution fusion | flops 16908288 | bytes 1130624 | tf_op jit(solution)/shard_map/dot_general | solution.py:921
  82.2 14.7 %all-to-all-done.2 = bf16[32,136,128]{2,1,0:T(8,128)(2,1)S(1)} async-done(((bf16[32,136,128]{2,1,0:T(8,128)(2,1)}), bf16[32,136,128]{2,1,0:T(8,128)(2,1)S(1)}, u32[]{:S(2)}, u32[]{:S(2)}) %all-to-all-start.2) | async-done | bytes 1114144 | tf_op jit(solution)/shard_map/all_to_all | solution.py:877
  96.9 6.6 %conditional.1 = (bf16[16,132,2,256]{3,2,1,0:T(2,128)(2,1)}, bf16[8,16,256]{2,1,0:T(8,128)(2,1)S(1)}) conditional(s32[]{:T(128)} %convert_element_type.45, (s32[]{:T(128)}, s32[16,4]{0,1:T(4,128)}, s32[512]{0:T(512)S(1)}, bf16[64,64,2,256]{3,2,1,0:T(2,128)(2,1)}, s32[512]{0:T(512)S(1)}, /*index=5*/s32[512]{0:T(512)S(1)}, s32[512,128]{1,0:T(8,128)}, ...), branch_computations={%region_20.21_spmd, %region_21.22_spmd} | conditional | bytes 17391776 | solution.py:961
  96.9 6.6 %gather_attend.1 = (bf16[2112,4,128]{2,1,0:T(4,128)(2,1)}, bf16[8,16,256]{2,1,0:T(8,128)(2,1)S(1)}) custom-call(s32[16]{0:T(128)S(1)} %get-tuple-element.65.source_ref, s32[32]{0:T(128)S(1)} %get-tuple-element.66.beyond_ref, s32[32,128]{1,0:T(8,128)S(1)} %get-tuple-element.67.place_ref, bf16[16,8,128]{2,1,0:T(8,128)(2,1)S(1)} %copy.46.query_ref, ...), custom_call_target="tpu_custom_call" | custom-call | tf_op jit(solution)/shard_map/cond/branch_1_fun/gather_attend/pallas_call | solution.py:743
  103.5 14.0 %all_to_all.19 = bf16[8,16,256]{2,1,0:T(8,128)(2,1)S(1)} all-to-all(bf16[8,16,256]{2,1,0:T(8,128)(2,1)S(1)} %get-tuple-element.97), channel_id=1, replica_groups=mesh['head'=8,'blk'=32] {'head'}, dimensions={0} | all-to-all | bytes 131072 | tf_op jit(solution)/shard_map/all_to_all | solution.py:962
  117.5 0.6 add_convert_fusion
  (74 shorter events, 5.7 us)
Async XLA Ops:
  6.8 12.3 %copy-start = (s32[512]{0:T(512)S(1)}, s32[512]{0:T(512)}, u32[]{:S(2)}) copy-start(s32[512]{0:T(512)} %count_hbm.1) | copy-start | bytes 6148
  6.8 12.3 %copy-start.7 = (s32[512]{0:T(512)S(1)}, s32[512]{0:T(512)}, u32[]{:S(2)}) copy-start(s32[512]{0:T(512)} %param.17) | copy-start | bytes 6148
  6.9 15.3 %copy-start.2 = (s32[512]{0:T(512)S(1)}, s32[512]{0:T(512)}, u32[]{:S(2)}) copy-start(s32[512]{0:T(512)} %length_hbm.1) | copy-start | bytes 6148
  6.9 54.1 %all-to-all-start.1 = ((bf16[32,216,128]{2,1,0:T(8,128)(2,1)}), bf16[32,216,128]{2,1,0:T(8,128)(2,1)S(1)}, u32[]{:S(2)}, u32[]{:S(2)}) async-start(bf16[32,216,128]{2,1,0:T(8,128)(2,1)} %bitcast.63), calls=%async_computation.1 | async-start | bytes 3538944 | tf_op jit(solution)/shard_map/all_to_all | solution.py:877
  19.1 11.2 %copy-start.6 = (bf16[16,256]{1,0:T(8,128)(2,1)S(1)}, bf16[16,256]{1,0:T(8,128)(2,1)}, u32[]{:S(2)}) copy-start(bf16[16,256]{1,0:T(8,128)(2,1)} %param.12) | copy-start | bytes 24580
  63.8 33.0 %all-to-all-start.2 = ((bf16[32,136,128]{2,1,0:T(8,128)(2,1)}), bf16[32,136,128]{2,1,0:T(8,128)(2,1)S(1)}, u32[]{:S(2)}, u32[]{:S(2)}) async-start(bf16[32,136,128]{2,1,0:T(8,128)(2,1)} %bitcast.65), calls=%async_computation.2 | async-start | bytes 2228224 | tf_op jit(solution)/shard_map/all_to_all | solution.py:877
  77.8 3.7 %copy-start.4 = (bf16[256,2048]{1,0:T(8,128)(2,1)S(1)}, bf16[256,2048]{1,0:T(8,128)(2,1)}, u32[]{:S(2)}) copy-start(bf16[256,2048]{1,0:T(8,128)(2,1)} %copy.40) | copy-start | bytes 3145732
